TPU v7x, 256 devices: a whole 4x4x8 slice. The times are simulated.
256 devices in a mesh: tok: 32 (over x, y, core), blk: 8 (over z).
Axes of the slice: x: 4, y: 4, z: 8, core: 2. Of those that a mesh axis runs over, the one named last changes fastest.
Arguments:
- attn_out: bfloat16 [32768, 1536], P(('tok', 'blk')), may hold values from -6 to 6
- resid: bfloat16 [32768, 1536], P(('tok', 'blk')), may hold values from -6 to 6
- w_o: bfloat16 [1536, 1536], replicated, may hold values from -0.15625 to 0.15625
- norm1_gain: float32 [1536], replicated, may hold values from 0.1 to 1.9
- router_w: float32 [1536, 40], replicated, may hold values from -32 to 32
- route_slot: int32 [32768, 8], P(('tok', 'blk')), may hold values from 0 to 63, all different within a row; in each aligned block of 128 rows (0 to 127, 128 to 255, ...) at most 32 rows name the same one
- slot_expert: int32 [64], replicated, may hold values from 0 to 39, as said below
- keep: int32 [32768], P(('tok', 'blk')), may hold values 0 or 1
- w_gate: bfloat16 [64, 1536, 512], P('tok', 'blk'), may hold values from -0.15625 to 0.15625
- w_up: bfloat16 [64, 1536, 512], P('tok', 'blk'), may hold values from -0.15625 to 0.15625
- w_down: bfloat16 [64, 1536, 512], P('tok', 'blk'), may hold values from -0.25 to 0.25
- norm2_gain: float32 [1536], replicated, may hold values from 0.1 to 1.9
Outputs:
- layer_out: bfloat16 [32768, 1536], P(('tok', 'blk'))
Inputs may be any that keep to these rules, and one draw needn't show every extreme that they name: `route_slot`: each row names 8 different slots; among the 128 rows of one device (aligned blocks of rows), no slot is named more than 32 times, a bound that some block reaches. `slot_expert`: every expert is named by one slot or more.
All inputs are finite; a program needn't handle non-finite values. No bound on the sum of `keep` on one device may be relied on, other than what follows from the above.
Results may differ from a plain program's by a relative error of at most 0.0099.
Values may be sent and summed in bfloat16 or wider, within the bound.
No kernel may reach another device: no remote copies, remote signals or barrier semaphores. Data moves between devices by JAX's collectives and lax.ppermute only.
A program may use at most 128 MiB of HBM per device.

v0:
```python
import jax
import jax.numpy as jnp
from jax import lax
from jax.sharding import PartitionSpec as P

eps = 1e-05


def rms_scale(values, gain):
    mean_sq = jnp.mean(values * values, axis=-1, keepdims=True)
    return values * lax.rsqrt(mean_sq + eps) * gain


def body(
    attn_out,
    resid,
    w_o,
    norm1_gain,
    router_w,
    route_slot,
    slot_expert,
    keep,
    w_gate,
    w_up,
    w_down,
    norm2_gain,
):
    rows, top = route_slot.shape
    width = resid.shape[1]
    slot_dev = w_gate.shape[0]
    groups = lax.axis_size("tok")
    slots = slot_dev * groups
    cap = max(2, 2 * rows * top // slots)
    hidden_state = resid.astype(jnp.float32) + jnp.dot(
        attn_out, w_o, preferred_element_type=jnp.float32
    )
    normed = rms_scale(hidden_state, norm1_gain).astype(jnp.bfloat16)
    logits = jnp.dot(normed.astype(jnp.float32), router_w, precision=lax.Precision.HIGHEST)
    slot_hits = route_slot[:, :, None] == jnp.arange(slots, dtype=jnp.int32)[None, None, :]
    expert_of = jnp.sum(jnp.where(slot_hits, slot_expert[None, None, :], 0), axis=-1)
    expert_hits = (
        expert_of[:, :, None] == jnp.arange(router_w.shape[1], dtype=jnp.int32)[None, None, :]
    )
    chosen = jnp.sum(jnp.where(expert_hits, logits[:, None, :], jnp.float32(0.0)), axis=-1)
    probs = jax.nn.softmax(chosen, axis=-1)
    live_rows = keep > 0
    live = jnp.repeat(live_rows, top)
    flat_hits = (slot_hits.reshape(rows * top, slots) & live[:, None]).astype(jnp.int32)
    before = jnp.cumsum(flat_hits, axis=0) - flat_hits
    position = jnp.sum(before * flat_hits, axis=1)
    flat_slot = route_slot.reshape(-1)
    owner = flat_slot // slot_dev
    local = flat_slot % slot_dev
    target_row = owner * cap + position
    target_local = jnp.where(live, local, slot_dev)
    token_index = jnp.arange(rows * top, dtype=jnp.int32) // top
    outgoing = jnp.zeros((slot_dev, groups * cap, width), jnp.bfloat16)
    outgoing = outgoing.at[target_local, target_row].set(normed[token_index], mode="drop")
    received = lax.all_to_all(outgoing, "tok", split_axis=1, concat_axis=1, tiled=True)
    gate_part = jnp.einsum(
        "snd,sdf->snf",
        received,
        lax.all_gather(w_gate, "blk", axis=1, tiled=True),
        preferred_element_type=jnp.float32,
    )
    up_part = jnp.einsum(
        "snd,sdf->snf",
        received,
        lax.all_gather(w_up, "blk", axis=1, tiled=True),
        preferred_element_type=jnp.float32,
    )
    act = (jax.nn.silu(gate_part) * up_part).astype(jnp.bfloat16)
    expert_y = jnp.einsum(
        "snf,sdf->snd",
        act,
        lax.all_gather(w_down, "blk", axis=1, tiled=True),
        preferred_element_type=jnp.float32,
    ).astype(jnp.bfloat16)
    returned = lax.all_to_all(expert_y, "tok", split_axis=1, concat_axis=1, tiled=True)
    picked = returned[local, target_row]
    scale = probs.reshape(-1) * live.astype(jnp.float32)
    moe = jnp.sum((picked.astype(jnp.float32) * scale[:, None]).reshape(rows, top, width), axis=1)
    mixed = hidden_state + moe
    return rms_scale(mixed, norm2_gain).astype(jnp.bfloat16)


def solution(mesh):
    placed = (
        P(("tok", "blk"), None),
        P(("tok", "blk"), None),
        P(),
        P(),
        P(),
        P(("tok", "blk"), None),
        P(),
        P(("tok", "blk")),
        P("tok", "blk", None),
        P("tok", "blk", None),
        P("tok", "blk", None),
        P(),
    )
    return jax.shard_map(
        body, mesh=mesh, in_specs=placed, out_specs=P(("tok", "blk"), None), check_vma=False
    )
```

profile of v0, /device:TPU:8, one launch (start us, length us, event | category | flops | bytes accessed | tf_op | source)
XLA Modules:
  0.0 326.5 jit_solution(14206349478592156242)
XLA Ops:
  6.5 0.7 all-gather.4.cloned.1.call-update
  7.3 0.7 all-gather.6.cloned.1.call-update
  8.0 0.7 broadcast_compare_fusion
  9.0 0.1 reshape.286
  9.1 0.8 copy.46
  10.4 18.0 %reduce-window.6 = s32[64,8,128]{2,1,0:T(8,128)S(1)} reduce-window(s32[64,8,128]{2,1,0:T(8,128)S(1)} %fusion.17, s32[]{:T(128)} %constant.56.clone.1), window={size=1x1x128 pad=0_0x0_0x127_0}, to_apply=%region_0.0 | reduce-window | flops 8323072 | bytes 524292 | tf_op jit(solution)/shard_map/reduce-window
  28.4 0.1 slice.12
  28.5 0.1 copy.50
  28.8 0.1 broadcast_add_fusion
  29.1 0.7 multiply_reduce_fusion.2
  29.9 0.8 and_reduce_fusion
  30.6 3.3 %multiply_reduce_fusion.1 = (f32[128]{0:T(128)S(1)}, f32[128,1536]{1,0:T(8,128)S(1)}) fusion(bf16[128,1536]{1,0:T(8,128)(2,1)S(1)} %copy-done, bf16[1536,1536]{1,0:T(8,128)(2,1)} %param.14, bf16[128,1536]{1,0:T(8,128)(2,1)} %param.13), kind=kOutput, calls=%fused_computation.18 | convolution fusion | flops 604766080 | bytes 6291968 | tf_op jit(solution)/shard_map/dot_general | solution.py:34
  34.0 0.9 copy-done.2
  34.9 0.1 multiply_convert_fusion.2
  35.0 19.7 %scatter_custom_fusion = bf16[2048,1536]{1,0:T(8,128)(2,1)} fusion(s32[1024]{0:T(1024)S(1)} %get-tuple-element.13, bf16[128,1536]{1,0:T(8,128)(2,1)S(1)} %multiply_convert_fusion.2, s32[1024]{0:T(1024)S(1)} %get-tuple-element.12, bf16[]{:T(256)} %constant.55.clone.1), kind=kCustom, calls=%fused_computation.11 | custom fusion | bytes 6291458
  54.7 12.7 %copy.52 = bf16[2,1024,1536]{2,0,1:T(2,128)(2,1)} copy(bf16[2,1024,1536]{2,1,0:T(8,128)(2,1)} %bitcast.34) | data formatting | bytes 12582912 | tf_op jit(solution)/shard_map/scatter | solution.py:58
  67.5 7.6 %all-to-all-start = ((bf16[2,1024,1536]{2,0,1:T(2,128)(2,1)}), bf16[2,1024,1536]{2,0,1:T(2,128)(2,1)}, u32[]{:S(2)}, u32[]{:S(2)}) async-start(bf16[2,1024,1536]{2,0,1:T(2,128)(2,1)} %copy.52), calls=%async_computation | async-start | bytes 12582912 | tf_op jit(solution)/shard_map/all_to_all | solution.py:59
  75.1 0.7 all-gather.8.cloned.1.call-update
  75.8 86.8 %all-to-all-done = bf16[2,1024,1536]{2,0,1:T(2,128)(2,1)} async-done(((bf16[2,1024,1536]{2,0,1:T(2,128)(2,1)}), bf16[2,1024,1536]{2,0,1:T(2,128)(2,1)}, u32[]{:S(2)}, u32[]{:S(2)}) %all-to-all-start) | async-done | bytes 6291488 | tf_op jit(solution)/shard_map/all_to_all | solution.py:59
  162.6 9.1 %fusion.3 = f32[2,1024,512]{2,1,0:T(8,128)} fusion(bf16[2,1536,512]{2,1,0:T(8,128)(2,1)} %all-gather.4.cloned.1.call-done, bf16[2,1024,1536]{2,0,1:T(2,128)(2,1)} %all-to-all-done), kind=kOutput, calls=%fused_computation.7 | convolution fusion | flops 3221225472 | bytes 13631488 | tf_op jit(solution)/shard_map/snd,sdf->snf/dot_general | solution.py:60
  171.7 13.4 %convolution_convert_fusion = bf16[2,1024,1536]{2,1,0:T(8,128)(2,1)} fusion(bf16[2,1536,512]{2,1,0:T(8,128)(2,1)} %all-gather.8.cloned.1.call-done, f32[2,1024,512]{2,1,0:T(8,128)} %fusion.3, bf16[2,1536,512]{2,1,0:T(8,128)(2,1)} %all-gather.6.cloned.1.call-done, bf16[2,1024,1536]{2,0,1:T(2,128)(2,1)} %all-to-all-done), kind=kOutput, calls=%fused_computation.9 | convolution fusion | flops 6451888128 | bytes 23068672 | tf_op jit(solution)/shard_map/snf,sdf->snd/dot_general | solution.py:73
  185.1 12.7 %copy.55 = bf16[2,1024,1536]{2,0,1:T(2,128)(2,1)} copy(bf16[2,1024,1536]{2,1,0:T(8,128)(2,1)} %convolution_convert_fusion) | data formatting | bytes 12582912 | tf_op jit(solution)/shard_map/convert_element_type | solution.py:78
  197.8 5.1 %all-to-all-start.1 = ((bf16[2,1024,1536]{2,0,1:T(2,128)(2,1)}), bf16[2,1024,1536]{2,0,1:T(2,128)(2,1)}, u32[]{:S(2)}, u32[]{:S(2)}) async-start(bf16[2,1024,1536]{2,0,1:T(2,128)(2,1)} %copy.55), calls=%async_computation.1 | async-start | bytes 12582912 | tf_op jit(solution)/shard_map/all_to_all | solution.py:79
  203.0 0.1 select_reduce_fusion
  203.1 0.5 fusion.23
  203.7 0.7 copy.57
  204.4 86.5 %all-to-all-done.1 = bf16[2,1024,1536]{2,0,1:T(2,128)(2,1)} async-done(((bf16[2,1024,1536]{2,0,1:T(2,128)(2,1)}), bf16[2,1024,1536]{2,0,1:T(2,128)(2,1)}, u32[]{:S(2)}, u32[]{:S(2)}) %all-to-all-start.1) | async-done | bytes 6291488 | tf_op jit(solution)/shard_map/all_to_all | solution.py:79
  290.9 6.4 %copy.56 = bf16[2,1024,1536]{2,1,0:T(8,128)(2,1)} copy(bf16[2,1024,1536]{2,0,1:T(2,128)(2,1)} %all-to-all-done.1) | data formatting | bytes 12582912 | tf_op jit(solution)/shard_map/all_to_all | solution.py:79
  297.3 17.8 %gather_fusion = bf16[1024,1536]{1,0:T(8,128)(2,1)S(1)} fusion(bf16[2,1024,1536]{2,1,0:T(8,128)(2,1)} %copy.56, s32[1024]{0:T(1024)S(1)} %bitcast.33), kind=kCustom, calls=%fused_computation.1 | custom fusion | bytes 6299648 | tf_op jit(solution)/shard_map/gather | solution.py:80
  315.1 3.8 %fusion = f32[128,1536]{1,0:T(8,128)S(1)} fusion(bf16[1024,1536]{1,0:T(8,128)(2,1)S(1)} %gather_fusion, f32[128,8]{1,0:T(8,128)} %copy.57), kind=kLoop, calls=%fused_computation.4 | loop fusion | flops 4521984 | bytes 3936256 | tf_op jit(solution)/shard_map/reduce_sum | solution.py:82
  318.9 0.2 multiply_reduce_fusion
  319.1 0.9 multiply_convert_fusion.1
  (46 shorter events, 1.3 us)
Async XLA Ops:
  6.5 24.1 %copy-start = (bf16[128,1536]{1,0:T(8,128)(2,1)S(1)}, bf16[128,1536]{1,0:T(8,128)(2,1)}, u32[]{:S(2)}) copy-start(bf16[128,1536]{1,0:T(8,128)(2,1)} %param.12) | copy-start | bytes 1179652
  6.5 69.3 %all-gather.4.cloned.1.call-start = ((), (), s32[]{:S(2)}) async-start(), calls=%async_computation.2 | async-start | bytes 3538944 | tf_op jit(solution)/shard_map/all_gather | solution.py:63
  7.3 164.4 %all-gather.6.cloned.1.call-start = ((), (), s32[]{:S(2)}) async-start(), calls=%async_computation.3 | async-start | bytes 3538944 | tf_op jit(solution)/shard_map/all_gather | solution.py:69
  10.4 24.5 %copy-start.6 = (f32[1536]{0:T(1024)S(1)}, f32[1536]{0:T(1024)}, u32[]{:S(2)}) copy-start(f32[1536]{0:T(1024)} %param.15) | copy-start | bytes 18436
  34.0 0.9 copy-start.2
  67.5 95.2 %all-to-all-start = ((bf16[2,1024,1536]{2,0,1:T(2,128)(2,1)}), bf16[2,1024,1536]{2,0,1:T(2,128)(2,1)}, u32[]{:S(2)}, u32[]{:S(2)}) async-start(bf16[2,1024,1536]{2,0,1:T(2,128)(2,1)} %copy.52), calls=%async_computation | async-start | bytes 12582912 | tf_op jit(solution)/shard_map/all_to_all | solution.py:59
  75.0 96.7 %all-gather.8.cloned.1.call-start = ((), (), s32[]{:S(2)}) async-start(), calls=%async_computation.4 | async-start | bytes 3538944 | tf_op jit(solution)/shard_map/all_gather | solution.py:76
  197.8 5.1 %copy-start.5 = (s32[128,8]{0,1:T(8,128)S(1)}, s32[128,8]{0,1:T(8,128)}, u32[]{:S(2)}) copy-start(s32[128,8]{0,1:T(8,128)} %param.17) | copy-start | bytes 12292
  197.8 5.2 %copy-start.8 = (s32[64]{0:T(128)S(1)}, s32[64]{0:T(128)}, u32[]{:S(2)}) copy-start(s32[64]{0:T(128)} %param.18) | copy-start | bytes 772
  197.8 5.3 %copy-start.4 = (f32[1536,40]{0,1:T(8,128)S(1)}, f32[1536,40]{0,1:T(8,128)}, u32[]{:S(2)}) copy-start(f32[1536,40]{0,1:T(8,128)} %param.16) | copy-start | bytes 737284
  197.8 93.1 %all-to-all-start.1 = ((bf16[2,1024,1536]{2,0,1:T(2,128)(2,1)}), bf16[2,1024,1536]{2,0,1:T(2,128)(2,1)}, u32[]{:S(2)}, u32[]{:S(2)}) async-start(bf16[2,1024,1536]{2,0,1:T(2,128)(2,1)} %copy.55), calls=%async_computation.1 | async-start | bytes 12582912 | tf_op jit(solution)/shard_map/all_to_all | solution.py:79
  297.3 22.7 %copy-start.1 = (bf16[128,1536]{1,0:T(8,128)(2,1)S(1)}, bf16[128,1536]{1,0:T(8,128)(2,1)}, u32[]{:S(2)}) copy-start(bf16[128,1536]{1,0:T(8,128)(2,1)} %param.12) | copy-start | bytes 1179652
  315.1 3.8 %copy-start.3 = (f32[128,1536]{1,0:T(8,128)S(1)}, f32[128,1536]{1,0:T(8,128)}, u32[]{:S(2)}) copy-start(f32[128,1536]{1,0:T(8,128)} %copy-done.2) | copy-start | bytes 2359300
  315.1 4.0 %copy-start.7 = (f32[1536]{0:T(1024)S(1)}, f32[1536]{0:T(1024)}, u32[]{:S(2)}) copy-start(f32[1536]{0:T(1024)} %param.23) | copy-start | bytes 18436
Sparse Core Ops, SparseCore 0:
  9.2 47.8 all-gather.3
  58.9 43.6 all-gather.5
  104.3 43.6 all-gather.7
where the time goes:
time: 327 us
  waiting for transfers between devices  175 us (54%)
  local copies, waits for them, and re-layouts  73 us (22%)
  matrix products  26.3 us (8%)
  other arithmetic  25.7 us (8%)
  between operations  13.4 us (4%)
  starting transfers between devices  12.8 us (4%)
    all_to_all x1, waiting for transfers between devices, body(): lax.all_to_all(outgoing, 'tok', split_axis=1, concat_axis=1, tiled=True)  86.8 us
    all_to_all x1, waiting for transfers between devices, body(): lax.all_to_all(expert_y, 'tok', split_axis=1, concat_axis=1, tiled=True)  86.5 us
    unnamed x20, local copies, waits for them, and re-layouts  21.4 us
    another operation x3, other arithmetic  18.2 us
    gather x1, local copies, waits for them, and re-layouts, body(): picked = returned[local, target_row]  17.8 us
    dot_general x1, matrix products, body(): jnp.einsum('snf,sdf->snd', act, lax.all_gather(w_down, 'blk', axis=1, til...  13.4 us
    convert_element_type x1, local copies, waits for them, and re-layouts, body(): expert_y = jnp.einsum('snf,sdf->snd', act, lax.all_gather(w_down, 'blk',...  12.7 us
    scatter x1, local copies, waits for them, and re-layouts, body(): outgoing.at[target_local, target_row].set(normed[token_index], mode='drop')  12.7 us
  transfers between devices with their start and end apart: 5, of which 2 were waited for; matrix products, arithmetic and copies ran while one was open for 21% of the time, Pallas kernels for 0%

commit v1 on v0

v1 whole, which is shorter than its diff:
```python
import functools

import jax
import jax.numpy as jnp
from jax import lax
from jax.experimental import pallas as pl
from jax.experimental.pallas import tpu as pltpu
from jax.sharding import Mesh
from jax.sharding import PartitionSpec as P

EPS = 1e-05
D = 1536
FF = 512
TOP = 8
SLOTS = 64
ROWS = 128
CAP = 32
BLOCKS = 16
LOCAL = 4
CHUNK = D // 8
GROUP = 2 * CHUNK
F32 = jnp.float32
BF16 = jnp.bfloat16
VMEM_LIMIT = 56 * 1024 * 1024


def params(*semantics):
    return pltpu.CompilerParams(
        dimension_semantics=semantics or None, vmem_limit_bytes=VMEM_LIMIT
    )


def entry_kernel(
    attn_ref, resid_ref, wo_ref, gain_ref, router_ref, route_ref, expert_ref, keep_ref,
    hidden_ref, normed_ref, weight_ref,
):
    step = pl.program_id(0)
    width = wo_ref.shape[1]
    cols = pl.ds(step * width, width)
    hidden_ref[:, cols] = resid_ref[...].astype(F32) + jnp.dot(
        attn_ref[...], wo_ref[...], preferred_element_type=F32
    )

    @pl.when(step == pl.num_programs(0) - 1)
    def _():
        values = hidden_ref[...]
        mean_sq = jnp.mean(values * values, axis=-1, keepdims=True)
        normed = (values * lax.rsqrt(mean_sq + EPS) * gain_ref[...]).astype(BF16)
        normed_ref[...] = normed
        logits = jnp.dot(
            normed.astype(F32), router_ref[...], precision=lax.Precision.HIGHEST,
            preferred_element_type=F32,
        )
        experts = logits.shape[1]
        lanes = 128
        pick = lax.broadcasted_iota(jnp.int32, (experts, lanes), 0) == expert_ref[...]
        by_slot = jnp.dot(
            logits, pick.astype(F32), precision=lax.Precision.HIGHEST,
            preferred_element_type=F32,
        )
        slot = lax.broadcasted_iota(jnp.int32, (ROWS, lanes), 1)
        named = slot == route_ref[:, 0:1]
        for k in range(1, TOP):
            named = named | (slot == route_ref[:, k : k + 1])
        top = jnp.max(jnp.where(named, by_slot, -jnp.inf), axis=-1, keepdims=True)
        grown = jnp.where(named, jnp.exp(jnp.where(named, by_slot - top, 0.0)), 0.0)
        probs = grown / jnp.sum(grown, axis=-1, keepdims=True)
        live = jnp.where(keep_ref[...] > 0, probs, 0.0)
        weight_ref[...] = jnp.transpose(live)[:SLOTS]


def entry(attn_out, resid, w_o, gain, router_w, route_slot, slot_expert, keep):
    steps = 6
    width = D // steps
    whole = lambda shape: pl.BlockSpec(shape, lambda i: (0, 0))
    return pl.pallas_call(
        entry_kernel,
        grid=(steps,),
        in_specs=[
            whole((ROWS, D)),
            pl.BlockSpec((ROWS, width), lambda i: (0, i)),
            pl.BlockSpec((D, width), lambda i: (0, i)),
            whole((1, D)),
            whole(router_w.shape),
            whole((ROWS, TOP)),
            whole((1, 128)),
            whole((ROWS, 1)),
        ],
        out_specs=[whole((ROWS, D)), whole((ROWS, D)), whole((SLOTS, ROWS))],
        out_shape=[
            jax.ShapeDtypeStruct((ROWS, D), F32),
            jax.ShapeDtypeStruct((ROWS, D), BF16),
            jax.ShapeDtypeStruct((SLOTS, ROWS), F32),
        ],
        compiler_params=params("arbitrary"),
        name="entry",
    )(attn_out, resid, w_o, gain, router_w, route_slot, slot_expert, keep)


def compact_kernel(weight_ref, rows_ref, packed_ref, spread_ref, scale_ref):
    weight = weight_ref[0]
    hit = weight > 0.0
    earlier = (
        lax.broadcasted_iota(jnp.int32, (ROWS, ROWS), 0)
        < lax.broadcasted_iota(jnp.int32, (ROWS, ROWS), 1)
    ).astype(BF16)
    place = jnp.dot(hit.astype(BF16), earlier, preferred_element_type=F32)
    place = jnp.where(hit, place, -1.0)
    rank = lax.broadcasted_iota(jnp.int32, (CAP, ROWS), 0).astype(F32)
    picks = [rank == place[s : s + 1] for s in range(LOCAL)]
    scale_ref[:, 0] = jnp.stack(
        [
            jnp.sum(jnp.where(picks[s], weight[s : s + 1], 0.0), axis=1, keepdims=True)
            for s in range(LOCAL)
        ]
    )
    pick = jnp.concatenate([p.astype(F32) for p in picks], axis=0)
    spread_ref[0] = jnp.transpose(pick).astype(BF16)
    packed = jnp.dot(pick.astype(BF16), rows_ref[0], preferred_element_type=F32).astype(BF16)
    packed_ref[:, 0] = packed.reshape(LOCAL, CAP, D)


def compact(weight, rows):
    return pl.pallas_call(
        compact_kernel,
        grid=(BLOCKS,),
        in_specs=[
            pl.BlockSpec((1, LOCAL, ROWS), lambda b: (b, 0, 0)),
            pl.BlockSpec((1, ROWS, D), lambda b: (b, 0, 0)),
        ],
        out_specs=[
            pl.BlockSpec((LOCAL, 1, CAP, D), lambda b: (0, b, 0, 0)),
            pl.BlockSpec((1, ROWS, LOCAL * CAP), lambda b: (b, 0, 0)),
            pl.BlockSpec((LOCAL, 1, CAP, 1), lambda b: (0, b, 0, 0)),
        ],
        out_shape=[
            jax.ShapeDtypeStruct((LOCAL, BLOCKS, CAP, D), BF16),
            jax.ShapeDtypeStruct((BLOCKS, ROWS, LOCAL * CAP), BF16),
            jax.ShapeDtypeStruct((LOCAL, BLOCKS, CAP, 1), F32),
        ],
        compiler_params=params("arbitrary"),
        name="compact",
    )(weight, rows)


def hidden_units_kernel(packed_ref, gate_ref, up_ref, act_ref):
    rows = packed_ref[0].reshape(BLOCKS * CAP, D)
    gate = jnp.dot(rows, gate_ref[...].reshape(D, FF), preferred_element_type=F32)
    up = jnp.dot(rows, up_ref[...].reshape(D, FF), preferred_element_type=F32)
    act_ref[0] = (gate / (1.0 + jnp.exp(-gate)) * up).astype(BF16)


def hidden_units(packed, weights):
    def block(which):
        return pl.BlockSpec((1, 8, 1, 1, CHUNK, FF), lambda s: (s // 2, 0, which, s % 2, 0, 0))

    return pl.pallas_call(
        hidden_units_kernel,
        grid=(LOCAL,),
        in_specs=[pl.BlockSpec((1, BLOCKS, CAP, D), lambda s: (s, 0, 0, 0)), block(0), block(1)],
        out_specs=pl.BlockSpec((1, BLOCKS * CAP, FF), lambda s: (s, 0, 0)),
        out_shape=jax.ShapeDtypeStruct((LOCAL, BLOCKS * CAP, FF), BF16),
        compiler_params=params("arbitrary"),
        name="hidden_units",
    )(packed, weights, weights)


def spread_kernel(order_ref, act_ref, down_ref, scale_ref, spread_ref, send_ref, keep_ref, part_ref):
    for s in range(LOCAL):
        down = down_ref[s // 2, :, 0, s % 2].reshape(GROUP, FF)
        part = lax.dot_general(
            act_ref[s], down, (((1,), (1,)), ((), ())), preferred_element_type=F32
        )
        scale = scale_ref[s].reshape(BLOCKS * CAP, 1)
        part_ref[:, s] = (part * scale).astype(BF16).reshape(BLOCKS, CAP, GROUP)
    half = BLOCKS // 2
    for j in range(BLOCKS):
        b = order_ref[j]
        rows = part_ref[b].reshape(LOCAL * CAP, GROUP)
        out = jnp.dot(spread_ref[b], rows, preferred_element_type=F32).astype(BF16)
        if j < half:
            keep_ref[j] = out
        else:
            send_ref[j - half] = out


def spread_rows(order, act, weights, scale, spread, group):
    half = BLOCKS // 2
    full = lambda shape: pl.BlockSpec(shape, lambda i, o: (0,) * len(shape))
    return pl.pallas_call(
        spread_kernel,
        grid_spec=pltpu.PrefetchScalarGridSpec(
            num_scalar_prefetch=1,
            grid=(1,),
            in_specs=[
                full(act.shape),
                pl.BlockSpec((2, 2, 1, 2, CHUNK, FF), lambda i, o: (0, group, 2, 0, 0, 0)),
                full(scale.shape),
                full(spread.shape),
            ],
            out_specs=[full((half, ROWS, GROUP)), full((half, ROWS, GROUP))],
            scratch_shapes=[pltpu.VMEM((BLOCKS, LOCAL, CAP, GROUP), BF16)],
        ),
        out_shape=[jax.ShapeDtypeStruct((half, ROWS, GROUP), BF16)] * 2,
        compiler_params=params("arbitrary"),
        name="spread",
    )(order, act, weights, scale, spread)


def closing_kernel(hidden_ref, gain_ref, *refs):
    pairs, out_ref = refs[:-1], refs[-1]
    moe = jnp.concatenate(
        [
            pairs[2 * g][...].astype(F32) + pairs[2 * g + 1][...].astype(F32)
            for g in range(len(pairs) // 2)
        ],
        axis=1,
    )
    mixed = hidden_ref[...] + moe
    mean_sq = jnp.mean(mixed * mixed, axis=-1, keepdims=True)
    out_ref[...] = (mixed * lax.rsqrt(mean_sq + EPS) * gain_ref[...]).astype(BF16)


def closing(hidden, gain, pairs):
    return pl.pallas_call(
        closing_kernel,
        out_shape=jax.ShapeDtypeStruct((ROWS, D), BF16),
        compiler_params=params(),
        name="closing",
    )(hidden, gain, *pairs)


def near(i):
    return i ^ 1


def far(i):
    return 3 - i


def reach(first, i):
    other = far if first is near else near
    return [i, other(i), first(i), other(first(i))]


def links(turn):
    return [(i, turn(i)) for i in range(4)]


def add(a, b):
    return (a.astype(F32) + b.astype(F32)).astype(BF16)


def body(
    attn_out, resid, w_o, norm1_gain, router_w, route_slot, slot_expert, keep,
    w_gate, w_up, w_down, norm2_gain,
):
    joined = jnp.stack([w_gate, w_up, w_down])
    weights = lax.all_gather(joined, ("core", "blk"), axis=0, tiled=False)
    weights = weights.reshape(2, 8, 3, 2, CHUNK, FF)

    slot_row = jnp.full((1, 128), -1, jnp.int32).at[0, :SLOTS].set(slot_expert)
    hidden, normed, weight = entry(
        attn_out, resid, w_o, norm1_gain.reshape(1, D), router_w, route_slot, slot_row,
        keep.reshape(ROWS, 1),
    )
    plane = ("x", "y")
    weight = lax.all_to_all(
        weight.reshape(BLOCKS, LOCAL, ROWS), plane, split_axis=0, concat_axis=0, tiled=True
    )
    copies = jnp.broadcast_to(normed[None], (BLOCKS, ROWS, D))
    rows = lax.all_to_all(copies, plane, split_axis=0, concat_axis=0, tiled=True)
    packed, spread, scale = compact(weight, rows)
    act = hidden_units(packed, weights)

    x, y = lax.axis_index("x"), lax.axis_index("y")
    plans = [("x", near), ("x", far), ("y", near), ("y", far)]
    pairs = []
    for group, (axis, first) in enumerate(plans):
        if axis == "x":
            second_axis = "y"
            order = [4 * a + b for a in reach(first, x) for b in reach(first, y)]
        else:
            second_axis = "x"
            order = [4 * b + a for a in reach(first, y) for b in reach(first, x)]
        order = jnp.stack(order).astype(jnp.int32)
        send, kept = spread_rows(order, act, weights, scale, spread, group)
        other = far if first is near else near
        got = lax.ppermute(send, axis, links(first))
        send, kept = add(kept[4:], got[4:]), add(kept[:4], got[:4])
        got = lax.ppermute(send, axis, links(other))
        send, kept = add(kept[2:], got[2:]), add(kept[:2], got[:2])
        got = lax.ppermute(send, second_axis, links(first))
        send, kept = add(kept[1], got[1]), add(kept[0], got[0])
        got = lax.ppermute(send, second_axis, links(other))
        pairs += [kept, got]
    return closing(hidden, norm2_gain.reshape(1, D), pairs)


def solution(mesh):
    fine = Mesh(mesh.devices.reshape(4, 4, 2, 8), ("x", "y", "core", "blk"))
    rows = P(("x", "y", "core", "blk"), None)
    slots = P(("x", "y", "core"), "blk", None)
    placed = (
        rows, rows, P(), P(), P(), rows, P(), P(("x", "y", "core", "blk")),
        slots, slots, slots, P(),
    )
    return jax.shard_map(body, mesh=fine, in_specs=placed, out_specs=rows, check_vma=False)
```

time: 327 us -> 253 us (0.77)
  the two profiles are of different devices: /device:TPU:8 before, /device:TPU:6 now
where the time goes in v1:
time: 253 us; the launch traced here: 252 us
  waiting for transfers between devices  113 us (45%)
  Pallas kernels  59.6 us (24%)
  starting transfers between devices  33.4 us (13%)
  between operations  13.5 us (5%)
  blocking collectives  13.1 us (5%)
  local copies, waits for them, and re-layouts  12 us (5%)
  other arithmetic  7.7 us (3%)
    all_to_all x1, waiting for transfers between devices, body(): lax.all_to_all(copies, plane, split_axis=0, concat_axis=0, tiled=True)  88.5 us
    pallas_call x4, Pallas kernels, spread_rows(): pl.pallas_call(spread_kernel, grid_spec=pltpu.PrefetchScalarGridSpec(num_...  24 us
    pallas_call x1, Pallas kernels, compact(): pl.pallas_call(compact_kernel, grid=(BLOCKS,), in_specs=[pl.BlockSpec((1,...  14.1 us
    all_to_all x1, blocking collectives, body(): lax.all_to_all(weight.reshape(BLOCKS, LOCAL, ROWS), plane, split_axis=0,...  13.1 us
    ppermute x4, waiting for transfers between devices, body(): got = lax.ppermute(send, axis, links(first))  11.8 us
    pallas_call x1, Pallas kernels, hidden_units(): pl.pallas_call(hidden_units_kernel, grid=(LOCAL,), in_specs=[pl.BlockSpec...  11.4 us
    ppermute x4, starting transfers between devices, body(): got = lax.ppermute(send, axis, links(first))  11.2 us
    ppermute x4, starting transfers between devices, body(): got = lax.ppermute(send, axis, links(other))  8.93 us
  transfers between devices with their start and end apart: 18, of which 9 were waited for; matrix products, arithmetic and copies ran while one was open for 7% of the time, Pallas kernels for 16%

profile of v1, /device:TPU:6, one launch (start us, length us, event | category | flops | bytes accessed | tf_op | source)
XLA Modules:
  0.0 251.9 jit_solution(5942602536432947407)
XLA Ops:
  6.6 2.5 pad_maximum_fusion
  9.1 1.2 copy.16.router_ref
  10.2 0.7 copy.17.route_ref
  11.0 0.7 copy.18.keep_ref
  14.1 7.7 %entry.1 = (f32[128,1536]{1,0:T(8,128)}, bf16[128,1536]{1,0:T(8,128)(2,1)}, f32[64,128]{1,0:T(8,128)}) custom-call(bf16[128,1536]{1,0:T(8,128)(2,1)} %attn_ref.1, bf16[128,1536]{1,0:T(8,128)(2,1)} %resid_ref.1, bf16[1536,1536]{1,0:T(8,128)(2,1)} %wo_ref.1, f32[1,1536]{1,0:T(1,128)} %reshape.78.gain_ref, f32[1536,40]{1,0:T(8,128)} %copy.16.router_ref, ...), custom_call_target="tpu_custom_call" | custom-call | tf_op jit(solution)/shard_map/entry/pallas_call | solution.py:76
  21.8 13.1 %all_to_all.10.weight_ref = f32[16,4,128]{2,1,0:T(4,128)} all-to-all(f32[16,4,128]{2,1,0:T(4,128)} %bitcast.56), channel_id=1, replica_groups=mesh['x'=4,'y'=4,'core'=2,'blk'=8] {'x','y'}, dimensions={0} | all-to-all | bytes 65536 | tf_op jit(solution)/shard_map/all_to_all | solution.py:268
  35.0 4.3 %broadcast_in_dim.2 = bf16[16,128,1536]{2,1,0:T(8,128)(2,1)} broadcast(bf16[128,1536]{1,0:T(8,128)(2,1)} %get-tuple-element.33), dimensions={1,2} | broadcast | bytes 6684672 | tf_op jit(solution)/shard_map/broadcast_in_dim | solution.py:271
  39.3 6.5 %all-to-all-start.1 = ((bf16[16,128,1536]{2,1,0:T(8,128)(2,1)}), bf16[16,128,1536]{2,1,0:T(8,128)(2,1)}, u32[]{:S(2)}, u32[]{:S(2)}) async-start(bf16[16,128,1536]{2,1,0:T(8,128)(2,1)} %broadcast_in_dim.2), calls=%async_computation.1 | async-start | bytes 12582912 | tf_op jit(solution)/shard_map/all_to_all | solution.py:272
  46.5 88.5 %all-to-all-done.1.rows_ref = bf16[16,128,1536]{2,1,0:T(8,128)(2,1)} async-done(((bf16[16,128,1536]{2,1,0:T(8,128)(2,1)}), bf16[16,128,1536]{2,1,0:T(8,128)(2,1)}, u32[]{:S(2)}, u32[]{:S(2)}) %all-to-all-start.1) | async-done | bytes 6291488 | tf_op jit(solution)/shard_map/all_to_all | solution.py:272
  135.0 14.1 %compact.1 = (bf16[4,16,32,1536]{3,2,1,0:T(8,128)(2,1)}, bf16[16,128,128]{2,1,0:T(8,128)(2,1)}, f32[4,16,32,1]{3,2,1,0:T(8,128)}) custom-call(f32[16,4,128]{2,1,0:T(4,128)} %all_to_all.10.weight_ref, bf16[16,128,1536]{2,1,0:T(8,128)(2,1)} %all-to-all-done.1.rows_ref), custom_call_target="tpu_custom_call" | custom-call | tf_op jit(solution)/shard_map/compact/pallas_call | solution.py:124
  149.0 11.4 %hidden_units.1.act_ref = bf16[4,512,512]{2,1,0:T(8,128)(2,1)} custom-call(bf16[4,16,32,1536]{3,2,1,0:T(8,128)(2,1)} %get-tuple-element.34.packed_ref, bf16[2,8,3,2,192,512]{5,4,3,2,1,0:T(8,128)(2,1)} %bitcast.47, bf16[2,8,3,2,192,512]{5,4,3,2,1,0:T(8,128)(2,1)} %bitcast.48), custom_call_target="tpu_custom_call" | custom-call | tf_op jit(solution)/shard_map/hidden_units/pallas_call | solution.py:157
  160.5 6.0 %spread.7 = (bf16[8,128,384]{2,1,0:T(8,128)(2,1)}, bf16[8,128,384]{2,1,0:T(8,128)(2,1)}) custom-call(s32[16]{0:T(128)} %stack.164.order_ref, bf16[4,512,512]{2,1,0:T(8,128)(2,1)} %hidden_units.1.act_ref, bf16[2,8,3,2,192,512]{5,4,3,2,1,0:T(8,128)(2,1)} %bitcast.49, f32[4,16,32,1]{3,2,1,0:T(8,128)} %get-tuple-element.35.scale_ref, ...), custom_call_target="tpu_custom_call" | custom-call | tf_op jit(solution)/shard_map/spread/pallas_call | solution.py:190
  167.1 6.0 %spread.6 = (bf16[8,128,384]{2,1,0:T(8,128)(2,1)}, bf16[8,128,384]{2,1,0:T(8,128)(2,1)}) custom-call(s32[16]{0:T(128)} %stack.163.order_ref, bf16[4,512,512]{2,1,0:T(8,128)(2,1)} %hidden_units.1.act_ref, bf16[2,8,3,2,192,512]{5,4,3,2,1,0:T(8,128)(2,1)} %bitcast.50, f32[4,16,32,1]{3,2,1,0:T(8,128)} %get-tuple-element.35.scale_ref, ...), custom_call_target="tpu_custom_call" | custom-call | tf_op jit(solution)/shard_map/spread/pallas_call | solution.py:190
  173.1 7.2 %collective-permute-start.8 = (bf16[8,128,384]{2,1,0:T(8,128)(2,1)}, bf16[8,128,384]{2,1,0:T(8,128)(2,1)S(1)}, u32[]{:S(2)}, u32[]{:S(2)}) collective-permute-start(bf16[8,128,384]{2,1,0:T(8,128)(2,1)} %get-tuple-element.42), channel_id=1, source_target_pairs={{0,16},{16,0},{32,48},{48,32},{1,17},{17,1},{33,49},{49,33},{2,18}... | collective-permute-start | bytes 2359304 | tf_op jit(solution)/shard_map/ppermute | solution.py:289
  181.0 6.0 %spread.5 = (bf16[8,128,384]{2,1,0:T(8,128)(2,1)}, bf16[8,128,384]{2,1,0:T(8,128)(2,1)}) custom-call(s32[16]{0:T(128)} %stack.162.order_ref, bf16[4,512,512]{2,1,0:T(8,128)(2,1)} %hidden_units.1.act_ref, bf16[2,8,3,2,192,512]{5,4,3,2,1,0:T(8,128)(2,1)} %bitcast.51, f32[4,16,32,1]{3,2,1,0:T(8,128)} %get-tuple-element.35.scale_ref, ...), custom_call_target="tpu_custom_call" | custom-call | tf_op jit(solution)/shard_map/spread/pallas_call | solution.py:190
  187.6 6.1 %spread.4 = (bf16[8,128,384]{2,1,0:T(8,128)(2,1)}, bf16[8,128,384]{2,1,0:T(8,128)(2,1)}) custom-call(s32[16]{0:T(128)} %stack.150.order_ref, bf16[4,512,512]{2,1,0:T(8,128)(2,1)} %hidden_units.1.act_ref, bf16[2,8,3,2,192,512]{5,4,3,2,1,0:T(8,128)(2,1)} %bitcast.52, f32[4,16,32,1]{3,2,1,0:T(8,128)} %get-tuple-element.35.scale_ref, ...), custom_call_target="tpu_custom_call" | custom-call | tf_op jit(solution)/shard_map/spread/pallas_call | solution.py:190
  193.7 4.0 %collective-permute-start = (bf16[8,128,384]{2,1,0:T(8,128)(2,1)}, bf16[8,128,384]{2,1,0:T(8,128)(2,1)S(1)}, u32[]{:S(2)}, u32[]{:S(2)}) collective-permute-start(bf16[8,128,384]{2,1,0:T(8,128)(2,1)} %get-tuple-element.38), channel_id=1, source_target_pairs={{0,64},{64,0},{128,192},{192,128},{1,65},{65,1},{129,193},{193,129... | collective-permute-start | bytes 2359304 | tf_op jit(solution)/shard_map/ppermute | solution.py:289
  197.9 1.2 collective-permute-start.13
  199.4 2.6 %collective-permute-done.4 = bf16[8,128,384]{2,1,0:T(8,128)(2,1)S(1)} collective-permute-done((bf16[8,128,384]{2,1,0:T(8,128)(2,1)}, bf16[8,128,384]{2,1,0:T(8,128)(2,1)S(1)}, u32[]{:S(2)}, u32[]{:S(2)}) %collective-permute-start.4) | collective-permute-done | bytes 786464 | tf_op jit(solution)/shard_map/ppermute | solution.py:289
  202.2 4.9 %collective-permute-start.5 = (bf16[4,128,384]{2,1,0:T(8,128)(2,1)S(1)}, bf16[4,128,384]{2,1,0:T(8,128)(2,1)S(1)}, u32[]{:S(2)}, u32[]{:S(2)}) collective-permute-start(bf16[4,128,384]{2,1,0:T(8,128)(2,1)S(1)} %get-tuple-element.50), channel_id=1, source_target_pairs={{0,64},{64,0},{128,192},{192,128},{1,65},{65,1},{129,193},{193,129... | collective-permute-start | bytes 1179656 | tf_op jit(solution)/shard_map/ppermute | solution.py:291
  207.2 9.2 %collective-permute-done = bf16[8,128,384]{2,1,0:T(8,128)(2,1)S(1)} collective-permute-done((bf16[8,128,384]{2,1,0:T(8,128)(2,1)}, bf16[8,128,384]{2,1,0:T(8,128)(2,1)S(1)}, u32[]{:S(2)}, u32[]{:S(2)}) %collective-permute-start) | collective-permute-done | bytes 786464 | tf_op jit(solution)/shard_map/ppermute | solution.py:289
  216.5 2.7 %collective-permute-start.1 = (bf16[4,128,384]{2,1,0:T(8,128)(2,1)S(1)}, bf16[4,128,384]{2,1,0:T(8,128)(2,1)S(1)}, u32[]{:S(2)}, u32[]{:S(2)}) collective-permute-start(bf16[4,128,384]{2,1,0:T(8,128)(2,1)S(1)} %get-tuple-element.52), channel_id=1, source_target_pairs={{0,192},{64,128},{128,64},{192,0},{1,193},{65,129},{129,65},{193,1... | collective-permute-start | bytes 1179656 | tf_op jit(solution)/shard_map/ppermute | solution.py:291
  220.2 0.9 collective-permute-start.10
  221.1 1.9 collective-permute-done.5
  223.2 3.2 %collective-permute-done.1 = bf16[4,128,384]{2,1,0:T(8,128)(2,1)S(1)} collective-permute-done((bf16[4,128,384]{2,1,0:T(8,128)(2,1)S(1)}, bf16[4,128,384]{2,1,0:T(8,128)(2,1)S(1)}, u32[]{:S(2)}, u32[]{:S(2)}) %collective-permute-start.1) | collective-permute-done | bytes 393248 | tf_op jit(solution)/shard_map/ppermute | solution.py:291
  226.9 1.9 collective-permute-done.14
  229.5 0.8 collective-permute-start.15
  231.0 2.6 %collective-permute-start.11 = (bf16[128,384]{1,0:T(8,128)(2,1)S(1)}, bf16[128,384]{1,0:T(8,128)(2,1)S(1)}, u32[]{:S(2)}, u32[]{:S(2)}) collective-permute-start(bf16[128,384]{1,0:T(8,128)(2,1)S(1)} %get-tuple-element.63), channel_id=1, source_target_pairs={{0,192},{64,128},{128,64},{192,0},{1,193},{65,129},{129,65},{193,1... | collective-permute-start | bytes 294920 | tf_op jit(solution)/shard_map/ppermute | solution.py:295
  234.3 1.1 collective-permute-start.7
  236.8 2.1 collective-permute-done.7.refs_3_
  238.9 3.0 %collective-permute-done.3.refs_1_ = bf16[128,384]{1,0:T(8,128)(2,1)S(1)} collective-permute-done((bf16[128,384]{1,0:T(8,128)(2,1)S(1)}, bf16[128,384]{1,0:T(8,128)(2,1)S(1)}, u32[]{:S(2)}, u32[]{:S(2)}) %collective-permute-start.3) | collective-permute-done | bytes 98336 | tf_op jit(solution)/shard_map/ppermute | solution.py:295
  242.6 2.4 closing.1
  (68 shorter events, 11.7 us)
Async XLA Ops:
  6.5 2.5 copy-start.4
  6.5 142.5 %all-gather.3.cloned.1.call-start = ((), (), s32[]{:S(2)}) async-start(), calls=%async_computation.2 | async-start | bytes 20054016 | tf_op jit(solution)/shard_map/all_gather | solution.py:259
  6.5 3.7 %copy-start.11 = (s32[128,8]{0,1:T(8,128)S(1)}, s32[128,8]{0,1:T(8,128)}, u32[]{:S(2)}) copy-start(s32[128,8]{0,1:T(8,128)} %param.19) | copy-start | bytes 12292
  6.5 4.4 %copy-start.12 = (s32[128]{0:T(128)S(1)}, s32[128]{0:T(128)}, u32[]{:S(2)}) copy-start(s32[128]{0:T(128)} %param.21) | copy-start | bytes 1540
  6.5 5.2 %copy-start.9 = (f32[1536]{0:T(1024)S(1)}, f32[1536]{0:T(1024)}, u32[]{:S(2)}) copy-start(f32[1536]{0:T(1024)} %param.17) | copy-start | bytes 18436
  6.5 6.4 %copy-start.13 = (s32[64]{0:T(128)S(1)}, s32[64]{0:T(128)}, u32[]{:S(2)}) copy-start(s32[64]{0:T(128)} %param.20) | copy-start | bytes 772
  39.3 95.7 %all-to-all-start.1 = ((bf16[16,128,1536]{2,1,0:T(8,128)(2,1)}), bf16[16,128,1536]{2,1,0:T(8,128)(2,1)}, u32[]{:S(2)}, u32[]{:S(2)}) async-start(bf16[16,128,1536]{2,1,0:T(8,128)(2,1)} %broadcast_in_dim.2), calls=%async_computation.1 | async-start | bytes 12582912 | tf_op jit(solution)/shard_map/all_to_all | solution.py:272
  166.4 31.2 %collective-permute-start.12 = (bf16[8,128,384]{2,1,0:T(8,128)(2,1)}, bf16[8,128,384]{2,1,0:T(8,128)(2,1)S(1)}, u32[]{:S(2)}, u32[]{:S(2)}) collective-permute-start(bf16[8,128,384]{2,1,0:T(8,128)(2,1)} %get-tuple-element.44), channel_id=1, source_target_pairs={{0,48},{16,32},{32,16},{48,0},{1,49},{17,33},{33,17},{49,1},{2,50}... | collective-permute-start | bytes 2359304 | tf_op jit(solution)/shard_map/ppermute | solution.py:289
  173.1 26.0 %collective-permute-start.8 = (bf16[8,128,384]{2,1,0:T(8,128)(2,1)}, bf16[8,128,384]{2,1,0:T(8,128)(2,1)S(1)}, u32[]{:S(2)}, u32[]{:S(2)}) collective-permute-start(bf16[8,128,384]{2,1,0:T(8,128)(2,1)} %get-tuple-element.42), channel_id=1, source_target_pairs={{0,16},{16,0},{32,48},{48,32},{1,17},{17,1},{33,49},{49,33},{2,18}... | collective-permute-start | bytes 2359304 | tf_op jit(solution)/shard_map/ppermute | solution.py:289
  187.0 15.0 %collective-permute-start.4 = (bf16[8,128,384]{2,1,0:T(8,128)(2,1)}, bf16[8,128,384]{2,1,0:T(8,128)(2,1)S(1)}, u32[]{:S(2)}, u32[]{:S(2)}) collective-permute-start(bf16[8,128,384]{2,1,0:T(8,128)(2,1)} %get-tuple-element.40), channel_id=1, source_target_pairs={{0,192},{64,128},{128,64},{192,0},{1,193},{65,129},{129,65},{193,1... | collective-permute-start | bytes 2359304 | tf_op jit(solution)/shard_map/ppermute | solution.py:289
  187.6 10.1 %copy-start = (bf16[8,128,384]{2,1,0:T(8,128)(2,1)S(1)}, bf16[8,128,384]{2,1,0:T(8,128)(2,1)}, u32[]{:S(2)}) copy-start(bf16[8,128,384]{2,1,0:T(8,128)(2,1)} %get-tuple-element.43) | copy-start | bytes 2359300
  193.7 5.4 %copy-start.1 = (bf16[8,128,384]{2,1,0:T(8,128)(2,1)S(1)}, bf16[8,128,384]{2,1,0:T(8,128)(2,1)}, u32[]{:S(2)}) copy-start(bf16[8,128,384]{2,1,0:T(8,128)(2,1)} %get-tuple-element.41) | copy-start | bytes 2359300
  193.7 22.6 %collective-permute-start = (bf16[8,128,384]{2,1,0:T(8,128)(2,1)}, bf16[8,128,384]{2,1,0:T(8,128)(2,1)S(1)}, u32[]{:S(2)}, u32[]{:S(2)}) collective-permute-start(bf16[8,128,384]{2,1,0:T(8,128)(2,1)} %get-tuple-element.38), channel_id=1, source_target_pairs={{0,64},{64,0},{128,192},{192,128},{1,65},{65,1},{129,193},{193,129... | collective-permute-start | bytes 2359304 | tf_op jit(solution)/shard_map/ppermute | solution.py:289
  197.7 4.3 %copy-start.2 = (bf16[8,128,384]{2,1,0:T(8,128)(2,1)S(1)}, bf16[8,128,384]{2,1,0:T(8,128)(2,1)}, u32[]{:S(2)}) copy-start(bf16[8,128,384]{2,1,0:T(8,128)(2,1)} %get-tuple-element.39) | copy-start | bytes 2359300
  197.9 21.4 %collective-permute-start.13 = (bf16[4,128,384]{2,1,0:T(8,128)(2,1)S(1)}, bf16[4,128,384]{2,1,0:T(8,128)(2,1)S(1)}, u32[]{:S(2)}, u32[]{:S(2)}) collective-permute-start(bf16[4,128,384]{2,1,0:T(8,128)(2,1)S(1)} %get-tuple-element.46), channel_id=1, source_target_pairs={{0,16},{16,0},{32,48},{48,32},{1,17},{17,1},{33,49},{49,33},{2,18}... | collective-permute-start | bytes 1179656 | tf_op jit(solution)/shard_map/ppermute | solution.py:291
  199.1 17.3 %copy-start.3 = (bf16[8,128,384]{2,1,0:T(8,128)(2,1)S(1)}, bf16[8,128,384]{2,1,0:T(8,128)(2,1)}, u32[]{:S(2)}) copy-start(bf16[8,128,384]{2,1,0:T(8,128)(2,1)} %get-tuple-element.37) | copy-start | bytes 2359300
  199.3 20.8 %collective-permute-start.9 = (bf16[4,128,384]{2,1,0:T(8,128)(2,1)S(1)}, bf16[4,128,384]{2,1,0:T(8,128)(2,1)S(1)}, u32[]{:S(2)}, u32[]{:S(2)}) collective-permute-start(bf16[4,128,384]{2,1,0:T(8,128)(2,1)S(1)} %get-tuple-element.48), channel_id=1, source_target_pairs={{0,48},{16,32},{32,16},{48,0},{1,49},{17,33},{33,17},{49,1},{2,50}... | collective-permute-start | bytes 1179656 | tf_op jit(solution)/shard_map/ppermute | solution.py:291
  202.2 20.8 %collective-permute-start.5 = (bf16[4,128,384]{2,1,0:T(8,128)(2,1)S(1)}, bf16[4,128,384]{2,1,0:T(8,128)(2,1)S(1)}, u32[]{:S(2)}, u32[]{:S(2)}) collective-permute-start(bf16[4,128,384]{2,1,0:T(8,128)(2,1)S(1)} %get-tuple-element.50), channel_id=1, source_target_pairs={{0,64},{64,0},{128,192},{192,128},{1,65},{65,1},{129,193},{193,129... | collective-permute-start | bytes 1179656 | tf_op jit(solution)/shard_map/ppermute | solution.py:291
  216.5 9.8 %collective-permute-start.1 = (bf16[4,128,384]{2,1,0:T(8,128)(2,1)S(1)}, bf16[4,128,384]{2,1,0:T(8,128)(2,1)S(1)}, u32[]{:S(2)}, u32[]{:S(2)}) collective-permute-start(bf16[4,128,384]{2,1,0:T(8,128)(2,1)S(1)} %get-tuple-element.52), channel_id=1, source_target_pairs={{0,192},{64,128},{128,64},{192,0},{1,193},{65,129},{129,65},{193,1... | collective-permute-start | bytes 1179656 | tf_op jit(solution)/shard_map/ppermute | solution.py:291
  219.4 9.4 %collective-permute-start.14 = (bf16[2,128,384]{2,1,0:T(8,128)(2,1)S(1)}, bf16[2,128,384]{2,1,0:T(8,128)(2,1)S(1)}, u32[]{:S(2)}, u32[]{:S(2)}) collective-permute-start(bf16[2,128,384]{2,1,0:T(8,128)(2,1)S(1)} %get-tuple-element.54), channel_id=1, source_target_pairs={{0,192},{64,128},{128,64},{192,0},{1,193},{65,129},{129,65},{193,1... | collective-permute-start | bytes 589832 | tf_op jit(solution)/shard_map/ppermute | solution.py:293
  220.2 10.1 %collective-permute-start.10 = (bf16[2,128,384]{2,1,0:T(8,128)(2,1)S(1)}, bf16[2,128,384]{2,1,0:T(8,128)(2,1)S(1)}, u32[]{:S(2)}, u32[]{:S(2)}) collective-permute-start(bf16[2,128,384]{2,1,0:T(8,128)(2,1)S(1)} %get-tuple-element.56), channel_id=1, source_target_pairs={{0,64},{64,0},{128,192},{192,128},{1,65},{65,1},{129,193},{193,129... | collective-permute-start | bytes 589832 | tf_op jit(solution)/shard_map/ppermute | solution.py:293
  223.0 13.1 %copy-start.10 = (f32[1536]{0:T(1024)S(1)}, f32[1536]{0:T(1024)}, u32[]{:S(2)}) copy-start(f32[1536]{0:T(1024)} %param.25) | copy-start | bytes 18436
  223.1 10.5 %collective-permute-start.6 = (bf16[2,128,384]{2,1,0:T(8,128)(2,1)S(1)}, bf16[2,128,384]{2,1,0:T(8,128)(2,1)S(1)}, u32[]{:S(2)}, u32[]{:S(2)}) collective-permute-start(bf16[2,128,384]{2,1,0:T(8,128)(2,1)S(1)} %get-tuple-element.58), channel_id=1, source_target_pairs={{0,48},{16,32},{32,16},{48,0},{1,49},{17,33},{33,17},{49,1},{2,50}... | collective-permute-start | bytes 589832 | tf_op jit(solution)/shard_map/ppermute | solution.py:293
  226.5 8.9 %collective-permute-start.2 = (bf16[2,128,384]{2,1,0:T(8,128)(2,1)S(1)}, bf16[2,128,384]{2,1,0:T(8,128)(2,1)S(1)}, u32[]{:S(2)}, u32[]{:S(2)}) collective-permute-start(bf16[2,128,384]{2,1,0:T(8,128)(2,1)S(1)} %get-tuple-element.60), channel_id=1, source_target_pairs={{0,16},{16,0},{32,48},{48,32},{1,17},{17,1},{33,49},{49,33},{2,18}... | collective-permute-start | bytes 589832 | tf_op jit(solution)/shard_map/ppermute | solution.py:293
  229.5 7.3 %collective-permute-start.15 = (bf16[128,384]{1,0:T(8,128)(2,1)S(1)}, bf16[128,384]{1,0:T(8,128)(2,1)S(1)}, u32[]{:S(2)}, u32[]{:S(2)}) collective-permute-start(bf16[128,384]{1,0:T(8,128)(2,1)S(1)} %get-tuple-element.61), channel_id=1, source_target_pairs={{0,64},{64,0},{128,192},{192,128},{1,65},{65,1},{129,193},{193,129... | collective-permute-start | bytes 294920 | tf_op jit(solution)/shard_map/ppermute | solution.py:295
  231.0 5.8 %collective-permute-start.11 = (bf16[128,384]{1,0:T(8,128)(2,1)S(1)}, bf16[128,384]{1,0:T(8,128)(2,1)S(1)}, u32[]{:S(2)}, u32[]{:S(2)}) collective-permute-start(bf16[128,384]{1,0:T(8,128)(2,1)S(1)} %get-tuple-element.63), channel_id=1, source_target_pairs={{0,192},{64,128},{128,64},{192,0},{1,193},{65,129},{129,65},{193,1... | collective-permute-start | bytes 294920 | tf_op jit(solution)/shard_map/ppermute | solution.py:295
  234.3 4.6 %collective-permute-start.7 = (bf16[128,384]{1,0:T(8,128)(2,1)S(1)}, bf16[128,384]{1,0:T(8,128)(2,1)S(1)}, u32[]{:S(2)}, u32[]{:S(2)}) collective-permute-start(bf16[128,384]{1,0:T(8,128)(2,1)S(1)} %get-tuple-element.65), channel_id=1, source_target_pairs={{0,16},{16,0},{32,48},{48,32},{1,17},{17,1},{33,49},{49,33},{2,18}... | collective-permute-start | bytes 294920 | tf_op jit(solution)/shard_map/ppermute | solution.py:295
  236.1 5.8 %collective-permute-start.3 = (bf16[128,384]{1,0:T(8,128)(2,1)S(1)}, bf16[128,384]{1,0:T(8,128)(2,1)S(1)}, u32[]{:S(2)}, u32[]{:S(2)}) collective-permute-start(bf16[128,384]{1,0:T(8,128)(2,1)S(1)} %get-tuple-element.67), channel_id=1, source_target_pairs={{0,48},{16,32},{32,16},{48,0},{1,49},{17,33},{33,17},{49,1},{2,50}... | collective-permute-start | bytes 294920 | tf_op jit(solution)/shard_map/ppermute | solution.py:295
  236.7 5.2 %copy-start.5 = (bf16[128,384]{1,0:T(8,128)(2,1)}, bf16[128,384]{1,0:T(8,128)(2,1)S(1)}, u32[]{:S(2)}) copy-start(bf16[128,384]{1,0:T(8,128)(2,1)S(1)} %collective-permute-done.15.refs_7_) | copy-start | bytes 294916
  236.8 5.1 %copy-start.6 = (bf16[128,384]{1,0:T(8,128)(2,1)}, bf16[128,384]{1,0:T(8,128)(2,1)S(1)}, u32[]{:S(2)}) copy-start(bf16[128,384]{1,0:T(8,128)(2,1)S(1)} %collective-permute-done.11.refs_5_) | copy-start | bytes 294916
  238.9 3.0 %copy-start.7 = (bf16[128,384]{1,0:T(8,128)(2,1)}, bf16[128,384]{1,0:T(8,128)(2,1)S(1)}, u32[]{:S(2)}) copy-start(bf16[128,384]{1,0:T(8,128)(2,1)S(1)} %collective-permute-done.7.refs_3_) | copy-start | bytes 294916
  241.9 0.6 copy-start.8
Sparse Core Ops, SparseCore 0:
  9.2 108.2 all-gather.2

commit v2 on v1

--- a/solution.py
+++ b/solution.py
@@ -21,13 +21,46 @@
 GROUP = 2 * CHUNK
 F32 = jnp.float32
 BF16 = jnp.bfloat16
-VMEM_LIMIT = 56 * 1024 * 1024
-
-
-def params(*semantics):
+MIB = 1024 * 1024
+
+
+def params(mib, *semantics):
     return pltpu.CompilerParams(
-        dimension_semantics=semantics or None, vmem_limit_bytes=VMEM_LIMIT
-    )
+        dimension_semantics=semantics or None, vmem_limit_bytes=mib * MIB
+    )
+
+
+PLANS = (("x", "y", 1, 3), ("x", "y", 3, 1), ("y", "x", 1, 3), ("y", "x", 3, 1))
+
+
+def block_at(plan, x, y, j):
+    big, small, first, other = plan
+    bit = lambda n: (j >> n) & 1
+    low = bit(0) * other ^ bit(1) * first
+    high = bit(2) * other ^ bit(3) * first
+    if big == "x":
+        return 4 * (x ^ high) + (y ^ low)
+    return 4 * (x ^ low) + (y ^ high)
+
+
+def each(count, unroll, step):
+    def run(i, carry):
+        step(i)
+        return carry
+
+    lax.fori_loop(0, count, run, 0, unroll=unroll)
+
+
+def links(turn):
+    return [(i, i ^ turn) for i in range(4)]
+
+
+def gather_plane(own, plan):
+    big, small, first, other = plan
+    held = own[None]
+    for axis, turn in ((small, other), (small, first), (big, other)):
+        held = jnp.concatenate([held, lax.ppermute(held, axis, links(turn))])
+    return held, lax.ppermute(held, big, links(first))
 
 
 def entry_kernel(
@@ -46,7 +79,8 @@
         values = hidden_ref[...]
         mean_sq = jnp.mean(values * values, axis=-1, keepdims=True)
         normed = (values * lax.rsqrt(mean_sq + EPS) * gain_ref[...]).astype(BF16)
-        normed_ref[...] = normed
+        for group in range(len(PLANS)):
+            normed_ref[group] = normed[:, group * GROUP : (group + 1) * GROUP]
         logits = jnp.dot(
             normed.astype(F32), router_ref[...], precision=lax.Precision.HIGHEST,
             preferred_element_type=F32,
@@ -86,61 +120,74 @@
             whole((1, 128)),
             whole((ROWS, 1)),
         ],
-        out_specs=[whole((ROWS, D)), whole((ROWS, D)), whole((SLOTS, ROWS))],
+        out_specs=[
+            whole((ROWS, D)),
+            pl.BlockSpec((len(PLANS), ROWS, GROUP), lambda i: (0, 0, 0)),
+            whole((SLOTS, ROWS)),
+        ],
         out_shape=[
             jax.ShapeDtypeStruct((ROWS, D), F32),
-            jax.ShapeDtypeStruct((ROWS, D), BF16),
+            jax.ShapeDtypeStruct((len(PLANS), ROWS, GROUP), BF16),
             jax.ShapeDtypeStruct((SLOTS, ROWS), F32),
         ],
-        compiler_params=params("arbitrary"),
+        compiler_params=params(16, "arbitrary"),
         name="entry",
     )(attn_out, resid, w_o, gain, router_w, route_slot, slot_expert, keep)
 
 
-def compact_kernel(weight_ref, rows_ref, packed_ref, spread_ref, scale_ref):
-    weight = weight_ref[0]
-    hit = weight > 0.0
+def compact_kernel(place_ref, *refs):
+    weight_refs, row_refs = refs[:2], refs[2:10]
+    packed_ref, spread_ref, scale_ref, pick_ref = refs[10:]
+    x, y = place_ref[0], place_ref[1]
+    half = BLOCKS // 2
     earlier = (
         lax.broadcasted_iota(jnp.int32, (ROWS, ROWS), 0)
         < lax.broadcasted_iota(jnp.int32, (ROWS, ROWS), 1)
     ).astype(BF16)
-    place = jnp.dot(hit.astype(BF16), earlier, preferred_element_type=F32)
-    place = jnp.where(hit, place, -1.0)
     rank = lax.broadcasted_iota(jnp.int32, (CAP, ROWS), 0).astype(F32)
-    picks = [rank == place[s : s + 1] for s in range(LOCAL)]
-    scale_ref[:, 0] = jnp.stack(
-        [
-            jnp.sum(jnp.where(picks[s], weight[s : s + 1], 0.0), axis=1, keepdims=True)
-            for s in range(LOCAL)
-        ]
-    )
-    pick = jnp.concatenate([p.astype(F32) for p in picks], axis=0)
-    spread_ref[0] = jnp.transpose(pick).astype(BF16)
-    packed = jnp.dot(pick.astype(BF16), rows_ref[0], preferred_element_type=F32).astype(BF16)
-    packed_ref[:, 0] = packed.reshape(LOCAL, CAP, D)
-
-
-def compact(weight, rows):
+    def choose(ref, start, i):
+        b = block_at(PLANS[0], x, y, start + i)
+        weight = ref[i, 4 * x + y]
+        hit = weight > 0.0
+        place = jnp.dot(hit.astype(BF16), earlier, preferred_element_type=F32)
+        place = jnp.where(hit, place, -1.0)
+        picks = [rank == place[s : s + 1] for s in range(LOCAL)]
+        for s in range(LOCAL):
+            scale_ref[s, b] = jnp.sum(
+                jnp.where(picks[s], weight[s : s + 1], 0.0), axis=1, keepdims=True
+            )
+        pick = jnp.concatenate([p.astype(F32) for p in picks], axis=0)
+        spread_ref[b] = jnp.transpose(pick).astype(BF16)
+        pick_ref[b] = pick.astype(BF16)
+
+    def pack(ref, group, start, i):
+        b = block_at(PLANS[group], x, y, start + i)
+        packed = jnp.dot(pick_ref[b], ref[i], preferred_element_type=F32).astype(BF16)
+        packed_ref[:, b, :, group * GROUP : (group + 1) * GROUP] = packed.reshape(
+            LOCAL, CAP, GROUP
+        )
+
+    for n, ref in enumerate(weight_refs):
+        each(half, 2, functools.partial(choose, ref, n * half))
+    for n, ref in enumerate(row_refs):
+        each(half, 4, functools.partial(pack, ref, n // 2, n % 2 * half))
+
+
+def compact(place, weights, rows):
+    vmem = pl.BlockSpec(memory_space=pltpu.VMEM)
     return pl.pallas_call(
         compact_kernel,
-        grid=(BLOCKS,),
-        in_specs=[
-            pl.BlockSpec((1, LOCAL, ROWS), lambda b: (b, 0, 0)),
-            pl.BlockSpec((1, ROWS, D), lambda b: (b, 0, 0)),
-        ],
-        out_specs=[
-            pl.BlockSpec((LOCAL, 1, CAP, D), lambda b: (0, b, 0, 0)),
-            pl.BlockSpec((1, ROWS, LOCAL * CAP), lambda b: (b, 0, 0)),
-            pl.BlockSpec((LOCAL, 1, CAP, 1), lambda b: (0, b, 0, 0)),
-        ],
+        in_specs=[pl.BlockSpec(memory_space=pltpu.SMEM)] + [vmem] * 10,
+        out_specs=[vmem] * 3,
         out_shape=[
             jax.ShapeDtypeStruct((LOCAL, BLOCKS, CAP, D), BF16),
             jax.ShapeDtypeStruct((BLOCKS, ROWS, LOCAL * CAP), BF16),
             jax.ShapeDtypeStruct((LOCAL, BLOCKS, CAP, 1), F32),
         ],
-        compiler_params=params("arbitrary"),
+        scratch_shapes=[pltpu.VMEM((BLOCKS, LOCAL * CAP, ROWS), BF16)],
+        compiler_params=params(24),
         name="compact",
-    )(weight, rows)
+    )(place, *weights, *rows)
 
 
 def hidden_units_kernel(packed_ref, gate_ref, up_ref, act_ref):
@@ -160,12 +207,12 @@
         in_specs=[pl.BlockSpec((1, BLOCKS, CAP, D), lambda s: (s, 0, 0, 0)), block(0), block(1)],
         out_specs=pl.BlockSpec((1, BLOCKS * CAP, FF), lambda s: (s, 0, 0)),
         out_shape=jax.ShapeDtypeStruct((LOCAL, BLOCKS * CAP, FF), BF16),
-        compiler_params=params("arbitrary"),
+        compiler_params=params(24, "arbitrary"),
         name="hidden_units",
     )(packed, weights, weights)
 
 
-def spread_kernel(order_ref, act_ref, down_ref, scale_ref, spread_ref, send_ref, keep_ref, part_ref):
+def spread_kernel(plan, place_ref, act_ref, down_ref, scale_ref, spread_ref, send_ref, keep_ref, part_ref):
     for s in range(LOCAL):
         down = down_ref[s // 2, :, 0, s % 2].reshape(GROUP, FF)
         part = lax.dot_general(
@@ -174,21 +221,21 @@
         scale = scale_ref[s].reshape(BLOCKS * CAP, 1)
         part_ref[:, s] = (part * scale).astype(BF16).reshape(BLOCKS, CAP, GROUP)
     half = BLOCKS // 2
-    for j in range(BLOCKS):
-        b = order_ref[j]
+
+    def back(out_ref, start, i):
+        b = block_at(plan, place_ref[0], place_ref[1], start + i)
         rows = part_ref[b].reshape(LOCAL * CAP, GROUP)
-        out = jnp.dot(spread_ref[b], rows, preferred_element_type=F32).astype(BF16)
-        if j < half:
-            keep_ref[j] = out
-        else:
-            send_ref[j - half] = out
-
-
-def spread_rows(order, act, weights, scale, spread, group):
+        out_ref[i] = jnp.dot(spread_ref[b], rows, preferred_element_type=F32).astype(BF16)
+
+    each(half, 4, functools.partial(back, keep_ref, 0))
+    each(half, 4, functools.partial(back, send_ref, half))
+
+
+def spread_rows(place, act, weights, scale, spread, group):
     half = BLOCKS // 2
     full = lambda shape: pl.BlockSpec(shape, lambda i, o: (0,) * len(shape))
     return pl.pallas_call(
-        spread_kernel,
+        functools.partial(spread_kernel, PLANS[group]),
         grid_spec=pltpu.PrefetchScalarGridSpec(
             num_scalar_prefetch=1,
             grid=(1,),
@@ -202,9 +249,9 @@
             scratch_shapes=[pltpu.VMEM((BLOCKS, LOCAL, CAP, GROUP), BF16)],
         ),
         out_shape=[jax.ShapeDtypeStruct((half, ROWS, GROUP), BF16)] * 2,
-        compiler_params=params("arbitrary"),
+        compiler_params=params(24, "arbitrary"),
         name="spread",
-    )(order, act, weights, scale, spread)
+    )(place, act, weights, scale, spread)
 
 
 def closing_kernel(hidden_ref, gain_ref, *refs):
@@ -225,26 +272,9 @@
     return pl.pallas_call(
         closing_kernel,
         out_shape=jax.ShapeDtypeStruct((ROWS, D), BF16),
-        compiler_params=params(),
+        compiler_params=params(8),
         name="closing",
     )(hidden, gain, *pairs)
-
-
-def near(i):
-    return i ^ 1
-
-
-def far(i):
-    return 3 - i
-
-
-def reach(first, i):
-    other = far if first is near else near
-    return [i, other(i), first(i), other(first(i))]
-
-
-def links(turn):
-    return [(i, turn(i)) for i in range(4)]
 
 
 def add(a, b):
@@ -264,35 +294,24 @@
         attn_out, resid, w_o, norm1_gain.reshape(1, D), router_w, route_slot, slot_row,
         keep.reshape(ROWS, 1),
     )
-    plane = ("x", "y")
-    weight = lax.all_to_all(
-        weight.reshape(BLOCKS, LOCAL, ROWS), plane, split_axis=0, concat_axis=0, tiled=True
-    )
-    copies = jnp.broadcast_to(normed[None], (BLOCKS, ROWS, D))
-    rows = lax.all_to_all(copies, plane, split_axis=0, concat_axis=0, tiled=True)
-    packed, spread, scale = compact(weight, rows)
+    place = jnp.stack([lax.axis_index("x"), lax.axis_index("y")]).astype(jnp.int32)
+    slot_weights = gather_plane(weight.reshape(BLOCKS, LOCAL, ROWS), PLANS[0])
+    rows = []
+    for group, plan in enumerate(PLANS):
+        rows += gather_plane(normed[group], plan)
+    packed, spread, scale = compact(place, slot_weights, rows)
     act = hidden_units(packed, weights)
 
-    x, y = lax.axis_index("x"), lax.axis_index("y")
-    plans = [("x", near), ("x", far), ("y", near), ("y", far)]
     pairs = []
-    for group, (axis, first) in enumerate(plans):
-        if axis == "x":
-            second_axis = "y"
-            order = [4 * a + b for a in reach(first, x) for b in reach(first, y)]
-        else:
-            second_axis = "x"
-            order = [4 * b + a for a in reach(first, y) for b in reach(first, x)]
-        order = jnp.stack(order).astype(jnp.int32)
-        send, kept = spread_rows(order, act, weights, scale, spread, group)
-        other = far if first is near else near
-        got = lax.ppermute(send, axis, links(first))
+    for group, (big, small, first, other) in enumerate(PLANS):
+        send, kept = spread_rows(place, act, weights, scale, spread, group)
+        got = lax.ppermute(send, big, links(first))
         send, kept = add(kept[4:], got[4:]), add(kept[:4], got[:4])
-        got = lax.ppermute(send, axis, links(other))
+        got = lax.ppermute(send, big, links(other))
         send, kept = add(kept[2:], got[2:]), add(kept[:2], got[:2])
-        got = lax.ppermute(send, second_axis, links(first))
+        got = lax.ppermute(send, small, links(first))
         send, kept = add(kept[1], got[1]), add(kept[0], got[0])
-        got = lax.ppermute(send, second_axis, links(other))
+        got = lax.ppermute(send, small, links(other))
         pairs += [kept, got]
     return closing(hidden, norm2_gain.reshape(1, D), pairs)
 

time: 253 us -> 211 us (0.83)
  Pallas kernels: 59.6 us -> 32.6 us
  waiting for transfers between devices: 113 us -> 90.1 us
  blocking collectives: 13.1 us -> 0 us
  local copies, waits for them, and re-layouts: 12 us -> 24.3 us
  starting transfers between devices: 33.4 us -> 42.8 us
    all_to_all x1 -> x0, waiting for transfers between devices: 88.5 us -> none  [body(): lax.all_to_all(copies, plane, split_axis=0, concat_axis=0, tiled=True)]
    ppermute x16 -> x36, waiting for transfers between devices: 24 us -> 65.7 us  [the longest x15 30.9 us: gather_plane(): held = jnp.concatenate([held, lax.ppermute(held, axis, links(turn))])]
    all_gather x1, waiting for transfers between devices: 0.01 us -> 24.4 us  [body(): weights = lax.all_gather(joined, ('core', 'blk'), axis=0, tiled=False)]
    unnamed x30 -> x40, local copies, waits for them, and re-layouts: 2.6 us -> 24.1 us
    pallas_call x5, Pallas kernels: 38.1 us -> 19.8 us  [the longest x4 11.4 us: spread_rows(): pl.pallas_call(functools.partial(spread_kernel, PLANS[group]), grid_spec=...]
    ppermute x16 -> x36, starting transfers between devices: 26.8 us -> 42.8 us  [the longest x15 20.3 us: gather_plane(): held = jnp.concatenate([held, lax.ppermute(held, axis, links(turn))])]
    all_to_all x1 -> x0, blocking collectives: 13.1 us -> none  [body(): lax.all_to_all(weight.reshape(BLOCKS, LOCAL, ROWS), plane, split_axis=0,...]
    all_to_all x1 -> x0, starting transfers between devices: 6.54 us -> none  [body(): lax.all_to_all(copies, plane, split_axis=0, concat_axis=0, tiled=True)]
  transfers between devices with their start and end apart: 18 -> 37, of which waited for: 9 -> 18; matrix products, arithmetic and copies ran while one was open for 7% -> 2% of each run, Pallas kernels for 16% -> 10%
where the time goes in v2:
time: 211 us; the launch traced here: 210 us
  waiting for transfers between devices  90.1 us (43%)
  starting transfers between devices  42.8 us (20%)
  Pallas kernels  32.6 us (15%)
  local copies, waits for them, and re-layouts  24.3 us (12%)
  between operations  13.9 us (7%)
  other arithmetic  6.03 us (3%)
    ppermute x15, waiting for transfers between devices, gather_plane(): held = jnp.concatenate([held, lax.ppermute(held, axis, links(turn))])  30.9 us
    all_gather x1, waiting for transfers between devices, body(): weights = lax.all_gather(joined, ('core', 'blk'), axis=0, tiled=False)  24.4 us
    unnamed x40, local copies, waits for them, and re-layouts  24.1 us
    ppermute x15, starting transfers between devices, gather_plane(): held = jnp.concatenate([held, lax.ppermute(held, axis, links(turn))])  20.3 us
    ppermute x4, waiting for transfers between devices, body(): got = lax.ppermute(send, big, links(first))  17 us
    pallas_call x4, Pallas kernels, spread_rows(): pl.pallas_call(functools.partial(spread_kernel, PLANS[group]), grid_spec=...  11.4 us
    pallas_call x1, Pallas kernels, compact(): pl.pallas_call(compact_kernel, in_specs=[pl.BlockSpec(memory_space=pltpu....  8.4 us
    pallas_call x1, Pallas kernels, hidden_units(): pl.pallas_call(hidden_units_kernel, grid=(LOCAL,), in_specs=[pl.BlockSpec...  8.27 us
  transfers between devices with their start and end apart: 37, of which 18 were waited for; matrix products, arithmetic and copies ran while one was open for 2% of the time, Pallas kernels for 10%

profile of v2, /device:TPU:6, one launch (start us, length us, event | category | flops | bytes accessed | tf_op | source)
XLA Modules:
  0.0 209.7 jit_solution(18044602399759834622)
XLA Ops:
  6.5 2.4 %pad_maximum_fusion = bf16[3,2,192,512]{3,2,1,0:T(8,128)(2,1)} fusion(bf16[1,2,192,512]{3,2,1,0:T(8,128)(2,1)} %bitcast.36, bf16[1,2,192,512]{3,2,1,0:T(8,128)(2,1)} %bitcast.37, bf16[1,2,192,512]{3,2,1,0:T(8,128)(2,1)} %bitcast.38), kind=kLoop, calls=%fused_computation | loop fusion | flops 1179648 | bytes 2359296 | tf_op jit(solution)/shard_map/stack | solution.py:288
  11.7 2.3 %copy-done.4 = bf16[1536,1536]{1,0:T(8,128)(2,1)S(1)} copy-done((bf16[1536,1536]{1,0:T(8,128)(2,1)S(1)}, bf16[1536,1536]{1,0:T(8,128)(2,1)}, u32[]{:S(2)}) %copy-start.4) | copy-done | bytes 4718616
  14.1 3.5 %entry.1 = (f32[128,1536]{1,0:T(8,128)S(1)}, bf16[4,128,384]{2,1,0:T(8,128)(2,1)S(1)}, f32[64,128]{1,0:T(8,128)S(1)}) custom-call(bf16[128,1536]{1,0:T(8,128)(2,1)S(1)} %copy-done.11, bf16[128,1536]{1,0:T(8,128)(2,1)S(1)} %copy-done.12, bf16[1536,1536]{1,0:T(8,128)(2,1)S(1)} %copy-done.4, f32[1,1536]{1,0:T(1,128)S(1)} %reshape.74.gain_ref, ...), custom_call_target="tpu_custom_call" | custom-call | tf_op jit(solution)/shard_map/entry/pallas_call | solution.py:110
  21.3 2.2 %collective-permute-start.4 = (bf16[1,128,384]{2,1,0:T(8,128)(2,1)S(1)}, bf16[1,128,384]{2,1,0:T(8,128)(2,1)S(1)}, u32[]{:S(2)}, u32[]{:S(2)}) collective-permute-start(bf16[1,128,384]{2,1,0:T(8,128)(2,1)S(1)} %get-tuple-element.72), channel_id=1, source_target_pairs={{0,48},{16,32},{32,16},{48,0},{1,49},{17,33},{33,17},{49,1},{2,50}... | collective-permute-start | bytes 294920 | tf_op jit(solution)/shard_map/ppermute | solution.py:62
  23.5 2.2 %collective-permute-start.17 = (bf16[2,128,384]{2,1,0:T(8,128)(2,1)S(1)}, bf16[2,128,384]{2,1,0:T(8,128)(2,1)S(1)}, u32[]{:S(2)}, u32[]{:S(2)}) collective-permute-start(bf16[2,128,384]{2,1,0:T(8,128)(2,1)S(1)} %pad_maximum_fusion.13), channel_id=1, source_target_pairs={{0,192},{64,128},{128,64},{192,0},{1,193},{65,129},{129,65},{193,1... | collective-permute-start | bytes 589832 | tf_op jit(solution)/shard_map/ppermute | solution.py:62
  27.6 2.8 %collective-permute-done.17 = bf16[2,128,384]{2,1,0:T(8,128)(2,1)S(1)} collective-permute-done((bf16[2,128,384]{2,1,0:T(8,128)(2,1)S(1)}, bf16[2,128,384]{2,1,0:T(8,128)(2,1)S(1)}, u32[]{:S(2)}, u32[]{:S(2)}) %collective-permute-start.17) | collective-permute-done | bytes 196640 | tf_op jit(solution)/shard_map/ppermute | solution.py:62
  32.8 2.0 collective-permute-start.14
  37.6 6.2 %collective-permute-done.5 = bf16[2,128,384]{2,1,0:T(8,128)(2,1)S(1)} collective-permute-done((bf16[2,128,384]{2,1,0:T(8,128)(2,1)S(1)}, bf16[2,128,384]{2,1,0:T(8,128)(2,1)S(1)}, u32[]{:S(2)}, u32[]{:S(2)}) %collective-permute-start.5) | collective-permute-done | bytes 196640 | tf_op jit(solution)/shard_map/ppermute | solution.py:62
  43.9 2.2 %collective-permute-start.6 = (bf16[4,128,384]{2,1,0:T(8,128)(2,1)S(1)}, bf16[4,128,384]{2,1,0:T(8,128)(2,1)S(1)}, u32[]{:S(2)}, u32[]{:S(2)}) collective-permute-start(bf16[4,128,384]{2,1,0:T(8,128)(2,1)S(1)} %pad_maximum_fusion.5), channel_id=1, source_target_pairs={{0,192},{64,128},{128,64},{192,0},{1,193},{65,129},{129,65},{193,1... | collective-permute-start | bytes 1179656 | tf_op jit(solution)/shard_map/ppermute | solution.py:62
  49.4 7.8 %collective-permute-done.6 = bf16[4,128,384]{2,1,0:T(8,128)(2,1)S(1)} collective-permute-done((bf16[4,128,384]{2,1,0:T(8,128)(2,1)S(1)}, bf16[4,128,384]{2,1,0:T(8,128)(2,1)S(1)}, u32[]{:S(2)}, u32[]{:S(2)}) %collective-permute-start.6) | collective-permute-done | bytes 393248 | tf_op jit(solution)/shard_map/ppermute | solution.py:62
  57.8 7.2 %collective-permute-done.1 = f32[2,16,4,128]{3,2,1,0:T(4,128)S(1)} collective-permute-done((f32[2,16,4,128]{3,2,1,0:T(4,128)S(1)}, f32[2,16,4,128]{3,2,1,0:T(4,128)S(1)}, u32[]{:S(2)}, u32[]{:S(2)}) %collective-permute-start.1) | collective-permute-done | bytes 65568 | tf_op jit(solution)/shard_map/ppermute | solution.py:62
  66.2 6.8 %collective-permute-done.2 = f32[4,16,4,128]{3,2,1,0:T(4,128)S(1)} collective-permute-done((f32[4,16,4,128]{3,2,1,0:T(4,128)S(1)}, f32[4,16,4,128]{3,2,1,0:T(4,128)S(1)}, u32[]{:S(2)}, u32[]{:S(2)}) %collective-permute-start.2) | collective-permute-done | bytes 131104 | tf_op jit(solution)/shard_map/ppermute | solution.py:62
  73.2 6.4 %collective-permute-done.3.refs_1_ = f32[8,16,4,128]{3,2,1,0:T(4,128)} collective-permute-done((f32[8,16,4,128]{3,2,1,0:T(4,128)S(1)}, f32[8,16,4,128]{3,2,1,0:T(4,128)}, u32[]{:S(2)}, u32[]{:S(2)}) %collective-permute-start.3) | collective-permute-done | bytes 262176 | tf_op jit(solution)/shard_map/ppermute | solution.py:63
  81.9 8.4 %compact.1 = (bf16[4,16,32,1536]{3,2,1,0:T(8,128)(2,1)S(1)}, bf16[16,128,128]{2,1,0:T(8,128)(2,1)S(1)}, f32[4,16,32,1]{3,2,1,0:T(8,128)S(1)}) custom-call(s32[2]{0:T(128)S(1)} %pad_add_fusion.place_ref, f32[8,16,4,128]{3,2,1,0:T(4,128)S(1)} %pad_maximum_fusion.9.refs_0_, f32[8,16,4,128]{3,2,1,0:T(4,128)} %collective-permute-done.3.refs_1_, ...), custom_call_target="tpu_custom_call" | custom-call | tf_op jit(solution)/shard_map/compact/pallas_call | solution.py:178
  90.4 2.7 %copy-done.2 = bf16[4,16,32,1536]{3,2,1,0:T(8,128)(2,1)} copy-done((bf16[4,16,32,1536]{3,2,1,0:T(8,128)(2,1)}, bf16[4,16,32,1536]{3,2,1,0:T(8,128)(2,1)S(1)}, u32[]{:S(2)}) %copy-start.2) | copy-done | bytes 6291480
  93.0 24.4 %all-gather.3.cloned.1.call-done = bf16[48,2,192,512]{3,2,1,0:T(8,128)(2,1)} async-done(((bf16[3,2,192,512]{3,2,1,0:T(8,128)(2,1)}), bf16[48,2,192,512]{3,2,1,0:T(8,128)(2,1)}) %all-gather.3.cloned.1.call-update) | async-done | bytes 18874384 | tf_op jit(solution)/shard_map/all_gather | solution.py:289
  117.4 6.4 %copy-done = bf16[48,2,192,512]{3,2,1,0:T(8,128)(2,1)S(1)} copy-done((bf16[48,2,192,512]{3,2,1,0:T(8,128)(2,1)S(1)}, bf16[48,2,192,512]{3,2,1,0:T(8,128)(2,1)}, u32[]{:S(2)}) %copy-start) | copy-done | bytes 18874392
  123.8 2.8 %copy-done.3 = bf16[4,16,32,1536]{3,2,1,0:T(8,128)(2,1)S(1)} copy-done((bf16[4,16,32,1536]{3,2,1,0:T(8,128)(2,1)S(1)}, bf16[4,16,32,1536]{3,2,1,0:T(8,128)(2,1)}, u32[]{:S(2)}) %copy-start.3) | copy-done | bytes 6291480
  126.6 8.3 %hidden_units.1.act_ref = bf16[4,512,512]{2,1,0:T(8,128)(2,1)S(1)} custom-call(bf16[4,16,32,1536]{3,2,1,0:T(8,128)(2,1)S(1)} %copy-done.3, bf16[2,8,3,2,192,512]{5,4,3,2,1,0:T(8,128)(2,1)S(1)} %bitcast.26, bf16[2,8,3,2,192,512]{5,4,3,2,1,0:T(8,128)(2,1)S(1)} %bitcast.27), custom_call_target="tpu_custom_call" | custom-call | tf_op jit(solution)/shard_map/hidden_units/pallas_call | solution.py:204
  134.9 6.4 %copy-done.1 = bf16[48,2,192,512]{3,2,1,0:T(8,128)(2,1)S(1)} copy-done((bf16[48,2,192,512]{3,2,1,0:T(8,128)(2,1)S(1)}, bf16[48,2,192,512]{3,2,1,0:T(8,128)(2,1)}, u32[]{:S(2)}) %copy-start.1) | copy-done | bytes 18874392
  141.2 2.9 %spread.7 = (bf16[8,128,384]{2,1,0:T(8,128)(2,1)S(1)}, bf16[8,128,384]{2,1,0:T(8,128)(2,1)S(1)}) custom-call(s32[2]{0:T(128)S(1)} %pad_add_fusion.place_ref, bf16[4,512,512]{2,1,0:T(8,128)(2,1)S(1)} %hidden_units.1.act_ref, bf16[2,8,3,2,192,512]{5,4,3,2,1,0:T(8,128)(2,1)S(1)} %bitcast.28, f32[4,16,32,1]{3,2,1,0:T(8,128)S(1)} %get-tuple-element.35.scale_ref, ...), custom_call_target="tpu_custom_call" | custom-call | tf_op jit(solution)/shard_map/spread/pallas_call | solution.py:237
  144.1 2.8 %collective-permute-start.32 = (bf16[8,128,384]{2,1,0:T(8,128)(2,1)S(1)}, bf16[8,128,384]{2,1,0:T(8,128)(2,1)S(1)}, u32[]{:S(2)}, u32[]{:S(2)}) collective-permute-start(bf16[8,128,384]{2,1,0:T(8,128)(2,1)S(1)} %get-tuple-element.44), channel_id=1, source_target_pairs={{0,48},{16,32},{32,16},{48,0},{1,49},{17,33},{33,17},{49,1},{2,50}... | collective-permute-start | bytes 2359304 | tf_op jit(solution)/shard_map/ppermute | solution.py:308
  146.9 2.9 %spread.6 = (bf16[8,128,384]{2,1,0:T(8,128)(2,1)S(1)}, bf16[8,128,384]{2,1,0:T(8,128)(2,1)S(1)}) custom-call(s32[2]{0:T(128)S(1)} %pad_add_fusion.place_ref, bf16[4,512,512]{2,1,0:T(8,128)(2,1)S(1)} %hidden_units.1.act_ref, bf16[2,8,3,2,192,512]{5,4,3,2,1,0:T(8,128)(2,1)S(1)} %bitcast.29, f32[4,16,32,1]{3,2,1,0:T(8,128)S(1)} %get-tuple-element.35.scale_ref, ...), custom_call_target="tpu_custom_call" | custom-call | tf_op jit(solution)/shard_map/spread/pallas_call | solution.py:237
  150.1 2.9 %spread.5 = (bf16[8,128,384]{2,1,0:T(8,128)(2,1)S(1)}, bf16[8,128,384]{2,1,0:T(8,128)(2,1)S(1)}) custom-call(s32[2]{0:T(128)S(1)} %pad_add_fusion.place_ref, bf16[4,512,512]{2,1,0:T(8,128)(2,1)S(1)} %hidden_units.1.act_ref, bf16[2,8,3,2,192,512]{5,4,3,2,1,0:T(8,128)(2,1)S(1)} %bitcast.30, f32[4,16,32,1]{3,2,1,0:T(8,128)S(1)} %get-tuple-element.35.scale_ref, ...), custom_call_target="tpu_custom_call" | custom-call | tf_op jit(solution)/shard_map/spread/pallas_call | solution.py:237
  153.8 2.9 %spread.4 = (bf16[8,128,384]{2,1,0:T(8,128)(2,1)S(1)}, bf16[8,128,384]{2,1,0:T(8,128)(2,1)S(1)}) custom-call(s32[2]{0:T(128)S(1)} %pad_add_fusion.place_ref, bf16[4,512,512]{2,1,0:T(8,128)(2,1)S(1)} %hidden_units.1.act_ref, bf16[2,8,3,2,192,512]{5,4,3,2,1,0:T(8,128)(2,1)S(1)} %bitcast.31, f32[4,16,32,1]{3,2,1,0:T(8,128)S(1)} %get-tuple-element.35.scale_ref, ...), custom_call_target="tpu_custom_call" | custom-call | tf_op jit(solution)/shard_map/spread/pallas_call | solution.py:237
  157.6 7.5 %collective-permute-done.32 = bf16[8,128,384]{2,1,0:T(8,128)(2,1)S(1)} collective-permute-done((bf16[8,128,384]{2,1,0:T(8,128)(2,1)S(1)}, bf16[8,128,384]{2,1,0:T(8,128)(2,1)S(1)}, u32[]{:S(2)}, u32[]{:S(2)}) %collective-permute-start.32) | collective-permute-done | bytes 786464 | tf_op jit(solution)/shard_map/ppermute | solution.py:308
  165.7 4.6 %collective-permute-done.28 = bf16[8,128,384]{2,1,0:T(8,128)(2,1)S(1)} collective-permute-done((bf16[8,128,384]{2,1,0:T(8,128)(2,1)S(1)}, bf16[8,128,384]{2,1,0:T(8,128)(2,1)S(1)}, u32[]{:S(2)}, u32[]{:S(2)}) %collective-permute-start.28) | collective-permute-done | bytes 786464 | tf_op jit(solution)/shard_map/ppermute | solution.py:308
  170.6 3.1 %collective-permute-done.24 = bf16[8,128,384]{2,1,0:T(8,128)(2,1)S(1)} collective-permute-done((bf16[8,128,384]{2,1,0:T(8,128)(2,1)S(1)}, bf16[8,128,384]{2,1,0:T(8,128)(2,1)S(1)}, u32[]{:S(2)}, u32[]{:S(2)}) %collective-permute-start.24) | collective-permute-done | bytes 786464 | tf_op jit(solution)/shard_map/ppermute | solution.py:308
  176.1 4.2 %collective-permute-start.21 = (bf16[4,128,384]{2,1,0:T(8,128)(2,1)S(1)}, bf16[4,128,384]{2,1,0:T(8,128)(2,1)S(1)}, u32[]{:S(2)}, u32[]{:S(2)}) collective-permute-start(bf16[4,128,384]{2,1,0:T(8,128)(2,1)S(1)} %get-tuple-element.52), channel_id=1, source_target_pairs={{0,192},{64,128},{128,64},{192,0},{1,193},{65,129},{129,65},{193,1... | collective-permute-start | bytes 1179656 | tf_op jit(solution)/shard_map/ppermute | solution.py:310
  182.0 4.1 %collective-permute-done.25 = bf16[4,128,384]{2,1,0:T(8,128)(2,1)S(1)} collective-permute-done((bf16[4,128,384]{2,1,0:T(8,128)(2,1)S(1)}, bf16[4,128,384]{2,1,0:T(8,128)(2,1)S(1)}, u32[]{:S(2)}, u32[]{:S(2)}) %collective-permute-start.25) | collective-permute-done | bytes 393248 | tf_op jit(solution)/shard_map/ppermute | solution.py:310
  191.3 2.8 %collective-permute-start.31 = (bf16[128,384]{1,0:T(8,128)(2,1)S(1)}, bf16[128,384]{1,0:T(8,128)(2,1)S(1)}, u32[]{:S(2)}, u32[]{:S(2)}) collective-permute-start(bf16[128,384]{1,0:T(8,128)(2,1)S(1)} %get-tuple-element.63), channel_id=1, source_target_pairs={{0,192},{64,128},{128,64},{192,0},{1,193},{65,129},{129,65},{193,1... | collective-permute-start | bytes 294920 | tf_op jit(solution)/shard_map/ppermute | solution.py:314
  198.8 3.0 %collective-permute-done.23.refs_1_ = bf16[128,384]{1,0:T(8,128)(2,1)S(1)} collective-permute-done((bf16[128,384]{1,0:T(8,128)(2,1)S(1)}, bf16[128,384]{1,0:T(8,128)(2,1)S(1)}, u32[]{:S(2)}, u32[]{:S(2)}) %collective-permute-start.23) | collective-permute-done | bytes 98336 | tf_op jit(solution)/shard_map/ppermute | solution.py:314
  (127 shorter events, 39.1 us)
Async XLA Ops:
  6.5 110.9 %all-gather.3.cloned.1.call-start = ((), (), s32[]{:S(2)}) async-start(), calls=%async_computation | async-start | bytes 20054016 | tf_op jit(solution)/shard_map/all_gather | solution.py:289
  18.5 7.1 %collective-permute-start.12 = (bf16[1,128,384]{2,1,0:T(8,128)(2,1)S(1)}, bf16[1,128,384]{2,1,0:T(8,128)(2,1)S(1)}, u32[]{:S(2)}, u32[]{:S(2)}) collective-permute-start(bf16[1,128,384]{2,1,0:T(8,128)(2,1)S(1)} %get-tuple-element.70), channel_id=1, source_target_pairs={{0,192},{64,128},{128,64},{192,0},{1,193},{65,129},{129,65},{193,1... | collective-permute-start | bytes 294920 | tf_op jit(solution)/shard_map/ppermute | solution.py:62
  21.3 10.0 %collective-permute-start.4 = (bf16[1,128,384]{2,1,0:T(8,128)(2,1)S(1)}, bf16[1,128,384]{2,1,0:T(8,128)(2,1)S(1)}, u32[]{:S(2)}, u32[]{:S(2)}) collective-permute-start(bf16[1,128,384]{2,1,0:T(8,128)(2,1)S(1)} %get-tuple-element.72), channel_id=1, source_target_pairs={{0,48},{16,32},{32,16},{48,0},{1,49},{17,33},{33,17},{49,1},{2,50}... | collective-permute-start | bytes 294920 | tf_op jit(solution)/shard_map/ppermute | solution.py:62
  23.5 7.0 %collective-permute-start.17 = (bf16[2,128,384]{2,1,0:T(8,128)(2,1)S(1)}, bf16[2,128,384]{2,1,0:T(8,128)(2,1)S(1)}, u32[]{:S(2)}, u32[]{:S(2)}) collective-permute-start(bf16[2,128,384]{2,1,0:T(8,128)(2,1)S(1)} %pad_maximum_fusion.13), channel_id=1, source_target_pairs={{0,192},{64,128},{128,64},{192,0},{1,193},{65,129},{129,65},{193,1... | collective-permute-start | bytes 589832 | tf_op jit(solution)/shard_map/ppermute | solution.py:62
  25.7 7.1 %collective-permute-start.13 = (bf16[2,128,384]{2,1,0:T(8,128)(2,1)S(1)}, bf16[2,128,384]{2,1,0:T(8,128)(2,1)S(1)}, u32[]{:S(2)}, u32[]{:S(2)}) collective-permute-start(bf16[2,128,384]{2,1,0:T(8,128)(2,1)S(1)} %pad_maximum_fusion.12), channel_id=1, source_target_pairs={{0,64},{64,0},{128,192},{192,128},{1,65},{65,1},{129,193},{193,129... | collective-permute-start | bytes 589832 | tf_op jit(solution)/shard_map/ppermute | solution.py:62
  25.8 9.0 %collective-permute-start.9 = (bf16[2,128,384]{2,1,0:T(8,128)(2,1)S(1)}, bf16[2,128,384]{2,1,0:T(8,128)(2,1)S(1)}, u32[]{:S(2)}, u32[]{:S(2)}) collective-permute-start(bf16[2,128,384]{2,1,0:T(8,128)(2,1)S(1)} %pad_maximum_fusion.11), channel_id=1, source_target_pairs={{0,48},{16,32},{32,16},{48,0},{1,49},{17,33},{33,17},{49,1},{2,50}... | collective-permute-start | bytes 589832 | tf_op jit(solution)/shard_map/ppermute | solution.py:62
  30.5 15.5 %collective-permute-start.18 = (bf16[4,128,384]{2,1,0:T(8,128)(2,1)S(1)}, bf16[4,128,384]{2,1,0:T(8,128)(2,1)S(1)}, u32[]{:S(2)}, u32[]{:S(2)}) collective-permute-start(bf16[4,128,384]{2,1,0:T(8,128)(2,1)S(1)} %pad_maximum_fusion.8), channel_id=1, source_target_pairs={{0,16},{16,0},{32,48},{48,32},{1,17},{17,1},{33,49},{49,33},{2,18}... | collective-permute-start | bytes 1179656 | tf_op jit(solution)/shard_map/ppermute | solution.py:62
  31.3 12.5 %collective-permute-start.5 = (bf16[2,128,384]{2,1,0:T(8,128)(2,1)S(1)}, bf16[2,128,384]{2,1,0:T(8,128)(2,1)S(1)}, u32[]{:S(2)}, u32[]{:S(2)}) collective-permute-start(bf16[2,128,384]{2,1,0:T(8,128)(2,1)S(1)} %pad_maximum_fusion.10), channel_id=1, source_target_pairs={{0,16},{16,0},{32,48},{48,32},{1,17},{17,1},{33,49},{49,33},{2,18}... | collective-permute-start | bytes 589832 | tf_op jit(solution)/shard_map/ppermute | solution.py:62
  32.8 14.5 %collective-permute-start.14 = (bf16[4,128,384]{2,1,0:T(8,128)(2,1)S(1)}, bf16[4,128,384]{2,1,0:T(8,128)(2,1)S(1)}, u32[]{:S(2)}, u32[]{:S(2)}) collective-permute-start(bf16[4,128,384]{2,1,0:T(8,128)(2,1)S(1)} %pad_maximum_fusion.7), channel_id=1, source_target_pairs={{0,48},{16,32},{32,16},{48,0},{1,49},{17,33},{33,17},{49,1},{2,50}... | collective-permute-start | bytes 1179656 | tf_op jit(solution)/shard_map/ppermute | solution.py:62
  34.8 12.6 %collective-permute-start.10 = (bf16[4,128,384]{2,1,0:T(8,128)(2,1)S(1)}, bf16[4,128,384]{2,1,0:T(8,128)(2,1)S(1)}, u32[]{:S(2)}, u32[]{:S(2)}) collective-permute-start(bf16[4,128,384]{2,1,0:T(8,128)(2,1)S(1)} %pad_maximum_fusion.6), channel_id=1, source_target_pairs={{0,64},{64,0},{128,192},{192,128},{1,65},{65,1},{129,193},{193,129... | collective-permute-start | bytes 1179656 | tf_op jit(solution)/shard_map/ppermute | solution.py:62
  36.4 21.2 %collective-permute-start = (f32[1,16,4,128]{3,2,1,0:T(4,128)S(1)}, f32[1,16,4,128]{3,2,1,0:T(4,128)S(1)}, u32[]{:S(2)}, u32[]{:S(2)}) collective-permute-start(f32[1,16,4,128]{3,2,1,0:T(4,128)S(1)} %bitcast.32), channel_id=1, source_target_pairs={{0,48},{16,32},{32,16},{48,0},{1,49},{17,33},{33,17},{49,1},{2,50}... | collective-permute-start | bytes 98312 | tf_op jit(solution)/shard_map/ppermute | solution.py:62
  43.9 13.4 %collective-permute-start.6 = (bf16[4,128,384]{2,1,0:T(8,128)(2,1)S(1)}, bf16[4,128,384]{2,1,0:T(8,128)(2,1)S(1)}, u32[]{:S(2)}, u32[]{:S(2)}) collective-permute-start(bf16[4,128,384]{2,1,0:T(8,128)(2,1)S(1)} %pad_maximum_fusion.5), channel_id=1, source_target_pairs={{0,192},{64,128},{128,64},{192,0},{1,193},{65,129},{129,65},{193,1... | collective-permute-start | bytes 1179656 | tf_op jit(solution)/shard_map/ppermute | solution.py:62
  46.1 33.5 %collective-permute-start.19 = (bf16[8,128,384]{2,1,0:T(8,128)(2,1)S(1)}, bf16[8,128,384]{2,1,0:T(8,128)(2,1)}, u32[]{:S(2)}, u32[]{:S(2)}) collective-permute-start(bf16[8,128,384]{2,1,0:T(8,128)(2,1)S(1)} %pad_maximum_fusion.4.refs_8_), channel_id=1, source_target_pairs={{0,48},{16,32},{32,16},{48,0},{1,49},{17,33},{33,17},{49,1},{2,50}... | collective-permute-start | bytes 2359304 | tf_op jit(solution)/shard_map/ppermute | solution.py:63
  47.4 32.2 %collective-permute-start.15 = (bf16[8,128,384]{2,1,0:T(8,128)(2,1)S(1)}, bf16[8,128,384]{2,1,0:T(8,128)(2,1)}, u32[]{:S(2)}, u32[]{:S(2)}) collective-permute-start(bf16[8,128,384]{2,1,0:T(8,128)(2,1)S(1)} %pad_maximum_fusion.3.refs_6_), channel_id=1, source_target_pairs={{0,16},{16,0},{32,48},{48,32},{1,17},{17,1},{33,49},{49,33},{2,18}... | collective-permute-start | bytes 2359304 | tf_op jit(solution)/shard_map/ppermute | solution.py:63
  47.6 32.0 %collective-permute-start.11 = (bf16[8,128,384]{2,1,0:T(8,128)(2,1)S(1)}, bf16[8,128,384]{2,1,0:T(8,128)(2,1)}, u32[]{:S(2)}, u32[]{:S(2)}) collective-permute-start(bf16[8,128,384]{2,1,0:T(8,128)(2,1)S(1)} %pad_maximum_fusion.2.refs_4_), channel_id=1, source_target_pairs={{0,192},{64,128},{128,64},{192,0},{1,193},{65,129},{129,65},{193,1... | collective-permute-start | bytes 2359304 | tf_op jit(solution)/shard_map/ppermute | solution.py:63
  57.3 22.3 %collective-permute-start.7 = (bf16[8,128,384]{2,1,0:T(8,128)(2,1)S(1)}, bf16[8,128,384]{2,1,0:T(8,128)(2,1)}, u32[]{:S(2)}, u32[]{:S(2)}) collective-permute-start(bf16[8,128,384]{2,1,0:T(8,128)(2,1)S(1)} %pad_maximum_fusion.1.refs_2_), channel_id=1, source_target_pairs={{0,64},{64,0},{128,192},{192,128},{1,65},{65,1},{129,193},{193,129... | collective-permute-start | bytes 2359304 | tf_op jit(solution)/shard_map/ppermute | solution.py:63
  57.7 7.3 %collective-permute-start.1 = (f32[2,16,4,128]{3,2,1,0:T(4,128)S(1)}, f32[2,16,4,128]{3,2,1,0:T(4,128)S(1)}, u32[]{:S(2)}, u32[]{:S(2)}) collective-permute-start(f32[2,16,4,128]{3,2,1,0:T(4,128)S(1)} %pad_maximum_fusion.15), channel_id=1, source_target_pairs={{0,16},{16,0},{32,48},{48,32},{1,17},{17,1},{33,49},{49,33},{2,18}... | collective-permute-start | bytes 196616 | tf_op jit(solution)/shard_map/ppermute | solution.py:62
  65.0 8.0 %collective-permute-start.2 = (f32[4,16,4,128]{3,2,1,0:T(4,128)S(1)}, f32[4,16,4,128]{3,2,1,0:T(4,128)S(1)}, u32[]{:S(2)}, u32[]{:S(2)}) collective-permute-start(f32[4,16,4,128]{3,2,1,0:T(4,128)S(1)} %pad_maximum_fusion.14), channel_id=1, source_target_pairs={{0,192},{64,128},{128,64},{192,0},{1,193},{65,129},{129,65},{193,1... | collective-permute-start | bytes 393224 | tf_op jit(solution)/shard_map/ppermute | solution.py:62
  73.1 6.6 %collective-permute-start.3 = (f32[8,16,4,128]{3,2,1,0:T(4,128)S(1)}, f32[8,16,4,128]{3,2,1,0:T(4,128)}, u32[]{:S(2)}, u32[]{:S(2)}) collective-permute-start(f32[8,16,4,128]{3,2,1,0:T(4,128)S(1)} %pad_maximum_fusion.9.refs_0_), channel_id=1, source_target_pairs={{0,64},{64,0},{128,192},{192,128},{1,65},{65,1},{129,193},{193,129... | collective-permute-start | bytes 786440 | tf_op jit(solution)/shard_map/ppermute | solution.py:63
  144.1 21.0 %collective-permute-start.32 = (bf16[8,128,384]{2,1,0:T(8,128)(2,1)S(1)}, bf16[8,128,384]{2,1,0:T(8,128)(2,1)S(1)}, u32[]{:S(2)}, u32[]{:S(2)}) collective-permute-start(bf16[8,128,384]{2,1,0:T(8,128)(2,1)S(1)} %get-tuple-element.44), channel_id=1, source_target_pairs={{0,48},{16,32},{32,16},{48,0},{1,49},{17,33},{33,17},{49,1},{2,50}... | collective-permute-start | bytes 2359304 | tf_op jit(solution)/shard_map/ppermute | solution.py:308
  149.8 20.5 %collective-permute-start.28 = (bf16[8,128,384]{2,1,0:T(8,128)(2,1)S(1)}, bf16[8,128,384]{2,1,0:T(8,128)(2,1)S(1)}, u32[]{:S(2)}, u32[]{:S(2)}) collective-permute-start(bf16[8,128,384]{2,1,0:T(8,128)(2,1)S(1)} %get-tuple-element.42), channel_id=1, source_target_pairs={{0,16},{16,0},{32,48},{48,32},{1,17},{17,1},{33,49},{49,33},{2,18}... | collective-permute-start | bytes 2359304 | tf_op jit(solution)/shard_map/ppermute | solution.py:308
  153.0 20.7 %collective-permute-start.24 = (bf16[8,128,384]{2,1,0:T(8,128)(2,1)S(1)}, bf16[8,128,384]{2,1,0:T(8,128)(2,1)S(1)}, u32[]{:S(2)}, u32[]{:S(2)}) collective-permute-start(bf16[8,128,384]{2,1,0:T(8,128)(2,1)S(1)} %get-tuple-element.40), channel_id=1, source_target_pairs={{0,192},{64,128},{128,64},{192,0},{1,193},{65,129},{129,65},{193,1... | collective-permute-start | bytes 2359304 | tf_op jit(solution)/shard_map/ppermute | solution.py:308
  156.7 19.2 %collective-permute-start.20 = (bf16[8,128,384]{2,1,0:T(8,128)(2,1)S(1)}, bf16[8,128,384]{2,1,0:T(8,128)(2,1)S(1)}, u32[]{:S(2)}, u32[]{:S(2)}) collective-permute-start(bf16[8,128,384]{2,1,0:T(8,128)(2,1)S(1)} %get-tuple-element.38), channel_id=1, source_target_pairs={{0,64},{64,0},{128,192},{192,128},{1,65},{65,1},{129,193},{193,129... | collective-permute-start | bytes 2359304 | tf_op jit(solution)/shard_map/ppermute | solution.py:308
  165.3 14.9 %collective-permute-start.33 = (bf16[4,128,384]{2,1,0:T(8,128)(2,1)S(1)}, bf16[4,128,384]{2,1,0:T(8,128)(2,1)S(1)}, u32[]{:S(2)}, u32[]{:S(2)}) collective-permute-start(bf16[4,128,384]{2,1,0:T(8,128)(2,1)S(1)} %get-tuple-element.46), channel_id=1, source_target_pairs={{0,16},{16,0},{32,48},{48,32},{1,17},{17,1},{33,49},{49,33},{2,18}... | collective-permute-start | bytes 1179656 | tf_op jit(solution)/shard_map/ppermute | solution.py:310
  170.5 10.5 %collective-permute-start.29 = (bf16[4,128,384]{2,1,0:T(8,128)(2,1)S(1)}, bf16[4,128,384]{2,1,0:T(8,128)(2,1)S(1)}, u32[]{:S(2)}, u32[]{:S(2)}) collective-permute-start(bf16[4,128,384]{2,1,0:T(8,128)(2,1)S(1)} %get-tuple-element.48), channel_id=1, source_target_pairs={{0,48},{16,32},{32,16},{48,0},{1,49},{17,33},{33,17},{49,1},{2,50}... | collective-permute-start | bytes 1179656 | tf_op jit(solution)/shard_map/ppermute | solution.py:310
  173.9 12.1 %collective-permute-start.25 = (bf16[4,128,384]{2,1,0:T(8,128)(2,1)S(1)}, bf16[4,128,384]{2,1,0:T(8,128)(2,1)S(1)}, u32[]{:S(2)}, u32[]{:S(2)}) collective-permute-start(bf16[4,128,384]{2,1,0:T(8,128)(2,1)S(1)} %get-tuple-element.50), channel_id=1, source_target_pairs={{0,64},{64,0},{128,192},{192,128},{1,65},{65,1},{129,193},{193,129... | collective-permute-start | bytes 1179656 | tf_op jit(solution)/shard_map/ppermute | solution.py:310
  176.1 12.8 %collective-permute-start.21 = (bf16[4,128,384]{2,1,0:T(8,128)(2,1)S(1)}, bf16[4,128,384]{2,1,0:T(8,128)(2,1)S(1)}, u32[]{:S(2)}, u32[]{:S(2)}) collective-permute-start(bf16[4,128,384]{2,1,0:T(8,128)(2,1)S(1)} %get-tuple-element.52), channel_id=1, source_target_pairs={{0,192},{64,128},{128,64},{192,0},{1,193},{65,129},{129,65},{193,1... | collective-permute-start | bytes 1179656 | tf_op jit(solution)/shard_map/ppermute | solution.py:310
  180.4 10.7 %collective-permute-start.34 = (bf16[2,128,384]{2,1,0:T(8,128)(2,1)S(1)}, bf16[2,128,384]{2,1,0:T(8,128)(2,1)S(1)}, u32[]{:S(2)}, u32[]{:S(2)}) collective-permute-start(bf16[2,128,384]{2,1,0:T(8,128)(2,1)S(1)} %get-tuple-element.54), channel_id=1, source_target_pairs={{0,192},{64,128},{128,64},{192,0},{1,193},{65,129},{129,65},{193,1... | collective-permute-start | bytes 589832 | tf_op jit(solution)/shard_map/ppermute | solution.py:312
  181.1 10.1 %collective-permute-start.30 = (bf16[2,128,384]{2,1,0:T(8,128)(2,1)S(1)}, bf16[2,128,384]{2,1,0:T(8,128)(2,1)S(1)}, u32[]{:S(2)}, u32[]{:S(2)}) collective-permute-start(bf16[2,128,384]{2,1,0:T(8,128)(2,1)S(1)} %get-tuple-element.56), channel_id=1, source_target_pairs={{0,64},{64,0},{128,192},{192,128},{1,65},{65,1},{129,193},{193,129... | collective-permute-start | bytes 589832 | tf_op jit(solution)/shard_map/ppermute | solution.py:312
  186.2 7.9 %collective-permute-start.26 = (bf16[2,128,384]{2,1,0:T(8,128)(2,1)S(1)}, bf16[2,128,384]{2,1,0:T(8,128)(2,1)S(1)}, u32[]{:S(2)}, u32[]{:S(2)}) collective-permute-start(bf16[2,128,384]{2,1,0:T(8,128)(2,1)S(1)} %get-tuple-element.58), channel_id=1, source_target_pairs={{0,48},{16,32},{32,16},{48,0},{1,49},{17,33},{33,17},{49,1},{2,50}... | collective-permute-start | bytes 589832 | tf_op jit(solution)/shard_map/ppermute | solution.py:312
  189.0 6.8 %collective-permute-start.22 = (bf16[2,128,384]{2,1,0:T(8,128)(2,1)S(1)}, bf16[2,128,384]{2,1,0:T(8,128)(2,1)S(1)}, u32[]{:S(2)}, u32[]{:S(2)}) collective-permute-start(bf16[2,128,384]{2,1,0:T(8,128)(2,1)S(1)} %get-tuple-element.60), channel_id=1, source_target_pairs={{0,16},{16,0},{32,48},{48,32},{1,17},{17,1},{33,49},{49,33},{2,18}... | collective-permute-start | bytes 589832 | tf_op jit(solution)/shard_map/ppermute | solution.py:312
  191.3 5.9 %collective-permute-start.31 = (bf16[128,384]{1,0:T(8,128)(2,1)S(1)}, bf16[128,384]{1,0:T(8,128)(2,1)S(1)}, u32[]{:S(2)}, u32[]{:S(2)}) collective-permute-start(bf16[128,384]{1,0:T(8,128)(2,1)S(1)} %get-tuple-element.63), channel_id=1, source_target_pairs={{0,192},{64,128},{128,64},{192,0},{1,193},{65,129},{129,65},{193,1... | collective-permute-start | bytes 294920 | tf_op jit(solution)/shard_map/ppermute | solution.py:314
  (24 other events, 140.4 us)
Sparse Core Ops, SparseCore 0:
  9.2 108.1 all-gather.2
